TPU v7x, 256 devices: a whole 4x4x8 slice. The times are simulated.
256 devices in a mesh: row: 8 (over z_hi, core), col: 32 (over y, x, z_lo).
Axes of the slice: x: 4, y: 4, z: 8 (z_hi: 4, z_lo: 2; z = z_hi * 2 + z_lo), core: 2. Of those that a mesh axis runs over, the one named last changes fastest.
Arguments:
- tile_amps: bfloat16 [6144, 6144], P('row', 'col'), as said below
- cycle_ints: bfloat16 [6144, 6144], P('row', 'col'), as said below
- base_ints: bfloat16 [6144, 6144], P('row', 'col'), as said below
- amp_mask: int32 [96, 96], P('row', 'col'), may hold values from 0 to 1, as said below
- int_mask: int32 [96, 96], P('row', 'col'), may hold values from 0 to 1, as said below
- pair_amps: bfloat16 [64, 196608], P(None, ('row', 'col')), may hold values from -6 to 6
- ladder_ints: bfloat16 [196608, 1024], P(('row', 'col')), may hold values from -0.0546875 to 0.0546875
- pair_list: int32 [16], replicated, may hold values from 0 to 63, as said below
Outputs:
- cycle_residual: float32 [6144, 6144], P('row', 'col')
- ladder: float32 [16, 1024], P(None, 'col')
Inputs may be any that keep to these rules, and one draw needn't show every extreme that they name: `tile_amps`: equal to its transpose. `cycle_ints`: equal to its transpose. `base_ints`: equal to its transpose. `amp_mask`: 0 or 1, equal to its transpose, 1 on every diagonal tile. `int_mask`: 0 or 1, equal to its transpose, 1 on every diagonal tile. `pair_list`: distinct entries.
All inputs are finite; a program needn't handle non-finite values.
Results may differ from a plain program's by a relative error of at most 0.0029.
Values may be sent and summed in bfloat16 or wider, within the bound.
No kernel may reach another device: no remote copies, remote signals or barrier semaphores. Data moves between devices by JAX's collectives and lax.ppermute only.
A program may use at most 64 MiB of HBM per device.

v0:
```python
import jax
import jax.numpy as jnp
from jax import lax
from jax.sharding import PartitionSpec as P


def widen(mask, field):
    rows, cols = mask.shape
    tile = field.shape[0] // rows
    spread = jnp.broadcast_to(mask.astype(field.dtype)[:, None, :, None], (rows, tile, cols, tile))
    return field * spread.reshape(rows * tile, cols * tile)


def on_device(
    tile_amps, cycle_ints, base_ints, amp_mask, int_mask, pair_amps, ladder_ints, pair_list
):
    amplitudes = widen(amp_mask, tile_amps)
    integrals = widen(int_mask, cycle_ints)
    baseline = widen(int_mask, base_ints)
    amp_columns = lax.all_gather(amplitudes, "row", axis=0, tiled=True)
    section = amp_columns
    summed = baseline.astype(jnp.float32) + jnp.dot(
        lax.all_gather(integrals, "col", axis=1, tiled=True),
        section,
        preferred_element_type=jnp.float32,
    )
    intermediate = summed.astype(jnp.bfloat16)
    inter_columns = lax.all_gather(intermediate, "row", axis=0, tiled=True)
    section = inter_columns
    cycle_residual = jnp.dot(
        lax.all_gather(amplitudes, "col", axis=1, tiled=True),
        section,
        preferred_element_type=jnp.float32,
    )
    stored = pair_amps.shape[0]
    selector = (pair_list[:, None] == jnp.arange(stored, dtype=jnp.int32)[None, :]).astype(
        jnp.bfloat16
    )
    chosen = jnp.dot(selector, pair_amps, preferred_element_type=jnp.float32).astype(jnp.bfloat16)
    partial_sums = jnp.dot(chosen, ladder_ints, preferred_element_type=jnp.float32)
    totals = lax.psum(partial_sums, ("row", "col"))
    share_width = totals.shape[1] // lax.axis_size("col")
    ladder = lax.dynamic_slice_in_dim(totals, lax.axis_index("col") * share_width, share_width, 1)
    return (cycle_residual, ladder)


def solution(mesh):
    in_specs = (
        P("row", "col"),
        P("row", "col"),
        P("row", "col"),
        P("row", "col"),
        P("row", "col"),
        P(None, ("row", "col")),
        P(("row", "col"), None),
        P(),
    )
    out_specs = (P("row", "col"), P(None, "col"))
    return jax.shard_map(
        on_device, mesh=mesh, in_specs=in_specs, out_specs=out_specs, check_vma=False
    )
```

profile of v0, /device:TPU:1, one launch (start us, length us, event | category | flops | bytes accessed | tf_op | source)
XLA Modules:
  0.0 534.8 jit_solution(9945198933842615081)
XLA Ops:
  8.0 0.0 all-gather.9.cloned.1.call-start
  8.1 0.8 convert_element_type.17
  8.9 0.2 broadcast_in_dim.4
  9.0 0.5 reshape.14
  9.5 1.8 mul.12
  11.3 0.0 all-gather.7.cloned.1.call-start
  11.4 0.2 broadcast_in_dim.5
  11.6 0.5 reshape.15
  12.1 0.8 mul.14
  12.9 0.0 all-gather.7.cloned.1.call-update
  12.9 0.0 all-reduce.2.cloned.1.call-start
  13.0 1.1 fusion.1
  14.1 0.0 all-reduce.2.cloned.1.call-update
  14.1 0.0 all-gather.5.cloned.1.call-start
  14.2 0.7 all-gather.5.cloned.1.call-update
  14.9 0.0 all-gather.11.cloned.1.call-start
  14.9 39.0 %all-gather.9.cloned.1.call-done = bf16[6144,192]{0,1:T(8,128)(2,1)} async-done(((bf16[768,192]{0,1:T(8,128)(2,1)}), bf16[6144,192]{0,1:T(8,128)(2,1)}) %all-gather.9.cloned.1.call-update) | async-done | bytes 2359312 | tf_op jit(solution)/shard_map/all_gather | solution.py:20
  53.9 213.9 %all-gather.7.cloned.1.call-done = bf16[768,6144]{0,1:T(8,128)(2,1)} async-done(((bf16[768,192]{0,1:T(8,128)(2,1)}), bf16[768,6144]{0,1:T(8,128)(2,1)}) %all-gather.7.cloned.1.call-update) | async-done | bytes 9437200 | tf_op jit(solution)/shard_map/all_gather | solution.py:23
  267.8 7.1 %fusion = bf16[768,192]{0,1:T(8,128)(2,1)} fusion(bf16[6144,192]{0,1:T(8,128)(2,1)} %all-gather.9.cloned.1.call-done, bf16[768,6144]{0,1:T(8,128)(2,1)} %all-gather.7.cloned.1.call-done, bf16[768,192]{0,1:T(8,128)(2,1)S(1)} %copy-done.5, bf16[768,192]{0,1:T(8,128)(2,1)S(1)} %reshape.15), kind=kOutput, calls=%fused_computation.1 | convolution fusion | flops 1812529152 | bytes 12681216 | tf_op jit(solution)/shard_map/dot_general | solution.py:22
  275.0 101.3 %all-reduce.2.cloned.1.call-done = f32[16,1024]{1,0:T(8,128)} async-done(((f32[16,1024]{1,0:T(8,128)}), f32[16,1024]{1,0:T(8,128)}) %all-reduce.2.cloned.1.call-update) | async-done | bytes 65552 | tf_op jit(solution)/shard_map/psum | solution.py:41
  376.2 1.4 constant_dynamic-slice_fusion
  377.6 104.4 %all-gather.5.cloned.1.call-done = bf16[768,6144]{0,1:T(8,128)(2,1)} async-done(((bf16[768,192]{0,1:T(8,128)(2,1)}), bf16[768,6144]{0,1:T(8,128)(2,1)}) %all-gather.5.cloned.1.call-update) | async-done | bytes 9437200 | tf_op jit(solution)/shard_map/all_gather | solution.py:31
  482.0 38.5 %all-gather.11.cloned.1.call-done = bf16[6144,192]{0,1:T(8,128)(2,1)} async-done(((bf16[768,192]{0,1:T(8,128)(2,1)}), bf16[6144,192]{0,1:T(8,128)(2,1)}) %all-gather.11.cloned.1.call-update) | async-done | bytes 2359312 | tf_op jit(solution)/shard_map/all_gather | solution.py:28
  520.4 7.2 %fusion.4 = f32[768,192]{0,1:T(8,128)} fusion(bf16[6144,192]{0,1:T(8,128)(2,1)} %all-gather.11.cloned.1.call-done, bf16[768,6144]{0,1:T(8,128)(2,1)} %all-gather.5.cloned.1.call-done), kind=kOutput, calls=%fused_computation.7 | convolution fusion | flops 1811939328 | bytes 12386304 | tf_op jit(solution)/shard_map/dot_general | solution.py:30
  (15 shorter events, 0.1 us)
Async XLA Ops:
  8.0 5.0 copy-start
  8.0 3.4 copy-start.3
  8.0 45.9 %all-gather.9.cloned.1.call-start = ((), (), s32[]{:S(2)}) async-start(), calls=%async_computation.2 | async-start | bytes 2654208 | tf_op jit(solution)/shard_map/all_gather | solution.py:20
  8.9 3.2 copy-start.1
  9.5 3.5 copy-start.2
  9.5 3.5 copy-start.4
  11.3 256.5 %all-gather.7.cloned.1.call-start = ((), (), s32[]{:S(2)}) async-start(), calls=%async_computation.1 | async-start | bytes 9732096 | tf_op jit(solution)/shard_map/all_gather | solution.py:23
  11.6 256.2 %copy-start.5 = (bf16[768,192]{0,1:T(8,128)(2,1)S(1)}, bf16[768,192]{0,1:T(8,128)(2,1)}, u32[]{:S(2)}) copy-start(bf16[768,192]{0,1:T(8,128)(2,1)} %param.10) | copy-start | bytes 884740
  12.9 363.3 %all-reduce.2.cloned.1.call-start = ((), (), s32[]{:S(2)}) async-start(), calls=%async_computation.4 | async-start | bytes 131072 | tf_op jit(solution)/shard_map/psum | solution.py:41
  14.1 467.9 %all-gather.5.cloned.1.call-start = ((), (), s32[]{:S(2)}) async-start(), calls=%async_computation | async-start | bytes 9732096 | tf_op jit(solution)/shard_map/all_gather | solution.py:31
  14.9 505.6 %all-gather.11.cloned.1.call-start = ((), (), s32[]{:S(2)}) async-start(), calls=%async_computation.3 | async-start | bytes 2654208 | tf_op jit(solution)/shard_map/all_gather | solution.py:28
Sparse Core Ops, SparseCore 0:
  11.5 42.4 all-gather.8
  55.7 212.0 all-gather.6
  270.2 211.7 all-gather.4
  483.7 36.7 all-gather.10
Sparse Core Ops, SparseCore 1:
  18.9 357.3 all-reduce.1
where the time goes:
time: 535 us
  waiting for transfers between devices  498 us (93%)
  matrix products  15.4 us (3%)
  between operations  15.3 us (3%)
    all_gather x1, waiting for transfers between devices, on_device(): lax.all_gather(integrals, 'col', axis=1, tiled=True)  214 us
    all_gather x1, waiting for transfers between devices, on_device(): lax.all_gather(amplitudes, 'col', axis=1, tiled=True)  104 us
    psum x1, waiting for transfers between devices, on_device(): totals = lax.psum(partial_sums, ('row', 'col'))  101 us
    all_gather x1, waiting for transfers between devices, on_device(): amp_columns = lax.all_gather(amplitudes, 'row', axis=0, tiled=True)  39 us
    all_gather x1, waiting for transfers between devices, on_device(): inter_columns = lax.all_gather(intermediate, 'row', axis=0, tiled=True)  38.5 us
  transfers between devices with their start and end apart: 5, of which 5 were waited for; matrix products, arithmetic and copies ran while one was open for 2% of the time, Pallas kernels for 0%

commit v1 on v0

v1 whole, which is shorter than its diff:
```python
import functools

import jax
import jax.numpy as jnp
from jax import lax
from jax.experimental import pallas as pl
from jax.experimental.pallas import tpu as pltpu
from jax.sharding import PartitionSpec as P


TILE = 64
F32, BF16 = jnp.float32, jnp.bfloat16
STEPS = (0, -1, 1, 2)


def shift(value, zh=0, core=0, y=0, x=0, zl=0):
    pairs = []
    for r in range(8):
        for c in range(32):
            to_r = ((r // 2 + zh) % 4) * 2 + (r + core) % 2
            to_c = ((c // 8 + y) % 4) * 8 + ((c // 2 + x) % 4) * 2 + (c + zl) % 2
            pairs.append((r * 32 + c, to_r * 32 + to_c))
    return lax.ppermute(value, ("row", "col"), pairs)


def ring(value, axis):
    return [value] + [shift(value, **{axis: -step}) for step in STEPS[1:]]


def place():
    r, c = lax.axis_index("row"), lax.axis_index("col")
    return r // 2, r % 2, c // 8, (c // 2) % 4, c % 2


def swap_middle(t):
    low = lax.broadcasted_iota(jnp.int32, t[0].shape, 1) < TILE
    r = [pltpu.roll(v, TILE, 1) if i in (1, 2, 3, 4) else v for i, v in enumerate(t)]
    return [
        t[0],
        jnp.where(low, t[1], r[3]),
        jnp.where(low, r[3], r[4]),
        jnp.where(low, r[1], r[2]),
        jnp.where(low, r[2], t[4]),
        t[5],
    ]


def prepare_kernel(v_ref, a_ref, b_ref, im_ref, am_ref, va1, va2, b_out, keep, send_a, send_b):
    low = lax.broadcasted_iota(jnp.int32, (TILE, 128), 1) < TILE
    zl = lax.axis_index("col") % 2
    for which, (ref, mask) in enumerate(((v_ref, im_ref), (a_ref, am_ref), (b_ref, im_ref))):
        for k in range(3):
            tiles = []
            for t in range(6):
                block = ref[k * 64 : k * 64 + 64, t * 128 : t * 128 + 128].astype(F32)
                m = jnp.where(low, mask[k, 2 * t], mask[k, 2 * t + 1]).astype(F32)
                tiles.append(block * m)
            tiles = [v.astype(BF16) for v in swap_middle(tiles)]
            rows = slice(k * 64, k * 64 + 64)
            halves = (tiles[0:3], tiles[3:6])
            if which == 0:
                halves = [
                    [jnp.where(zl == 0, p, q) for p, q in zip(*pair)]
                    for pair in ((halves[1], halves[0]), (halves[0], halves[1]))
                ]
            for at, half in enumerate(halves):
                if which == 2:
                    continue
                for t, v in enumerate(half):
                    lanes = slice(t * 128, t * 128 + 128)
                    if k == 0:
                        va1[2 * which + at, 0:64, lanes] = v
                    elif k == 1:
                        va1[2 * which + at, 64:96, lanes] = v[0:32]
                        va2[2 * which + at, 0:32, lanes] = v[32:64]
                    else:
                        va2[2 * which + at, 32:96, lanes] = v
            if which > 0:
                into = keep if which == 1 else b_out
                for t in range(3):
                    lanes = slice(t * 128, t * 128 + 128)
                    into[rows, lanes] = jnp.where(zl == 0, tiles[t], tiles[t + 3])
                    (send_a if which == 1 else send_b)[rows, lanes] = jnp.where(zl == 0, tiles[t + 3], tiles[t])


VMEM = pl.BlockSpec(memory_space=pltpu.VMEM)
SMEM = pl.BlockSpec(memory_space=pltpu.SMEM)
ANY = pl.BlockSpec(memory_space=pl.ANY)


def prepare(vt, at, bt, int_mask, amp_mask):
    struct = jax.ShapeDtypeStruct
    return pl.pallas_call(
        prepare_kernel,
        name="prepare",
        out_shape=(
            struct((4, 96, 384), BF16),
            struct((4, 96, 384), BF16),
            struct((192, 384), BF16),
            struct((192, 384), BF16),
            struct((192, 384), BF16),
            struct((192, 384), BF16),
        ),
        in_specs=[VMEM, VMEM, VMEM, SMEM, SMEM],
        out_specs=(VMEM,) * 6,
        cost_estimate=pl.CostEstimate(flops=10**6, bytes_accessed=2 * 10**6, transcendentals=0),
    )(vt, at, bt, int_mask, amp_mask)


def stack_kernel(a, b, c, d, ints, amps, sem):
    copies = []
    for i, ref in enumerate((a, b, c, d)):
        for part in range(4):
            into = (ints, amps)[part // 2].at[i, part % 2]
            for lane in (0, 128, 256):
                lanes = pl.ds(lane, 128)
                copies.append(
                    pltpu.make_async_copy(ref.at[part, :, lanes], into.at[:, lanes], sem)
                )
    for copy in copies:
        copy.start()
    for copy in copies:
        copy.wait()


def stack(blocks):
    struct = jax.ShapeDtypeStruct
    return pl.pallas_call(
        stack_kernel,
        name="stack",
        out_shape=(struct((4, 2, 96, 384), BF16), struct((4, 2, 96, 384), BF16)),
        in_specs=[ANY] * 4,
        out_specs=(VMEM,) * 2,
        scratch_shapes=[pltpu.SemaphoreType.DMA],
        compiler_params=pltpu.CompilerParams(vmem_limit_bytes=4 << 20),
        cost_estimate=pl.CostEstimate(flops=1000, bytes_accessed=2 * 10**6, transcendentals=0),
    )(*blocks)


def product_kernel(stage, sending, *refs):
    stacks, pieces, (out, w, g, total, w_sems, g_sems) = refs[:8], refs[8:16], refs[16:]
    zh, core, y, x, _ = place()
    rows = slice(None) if stage == 1 else slice(192, 384) if sending else slice(0, 192)
    sides = ((0 if sending else 1),) if stage == 1 else (0, 1)

    @pl.loop(0, 4)
    def _(inner):
        di = jnp.where(inner < 2, 3 * inner, inner - 1)
        for outer, ds in enumerate(STEPS):
            for half in range(2):
                dy, dx = (ds, di) if half == 0 else (di, ds)
                at_y, at_x = lax.rem(y + dy + 4, 4), lax.rem(x + dx + 4, 4)
                row = pl.multiple_of((at_y * 4 + at_x) * 192 + half * 96, 32)
                for at, side in enumerate(sides):
                    for lane in (0, 128, 256):
                        pltpu.make_async_copy(
                            stacks[4 * half + outer].at[inner, side, :, pl.ds(lane, 128)],
                            w.at[pl.ds(row, 96), pl.ds(at * 384 + lane, 128)],
                            w_sems.at[at_y],
                        ).start()

    for i, dz in enumerate(STEPS):
        for other in range(2):
            at_z, at_core = lax.rem(zh + dz + 4, 4), lax.rem(core + other, 2)
            pltpu.make_async_copy(
                pieces[other * 4 + i].at[rows if stage == 2 else slice(0, 384)],
                g.at[at_z, :, pl.ds(pl.multiple_of(at_core * 384, 128), 384)],
                g_sems.at[at_z],
            ).start()
    total[...] = jnp.zeros_like(total)

    @pl.loop(0, 4)
    def _(k):
        part = pl.ds(pl.multiple_of(k * 768, 768), 768)
        pltpu.make_async_copy(w.at[part, :], w.at[part, :], w_sems.at[k]).wait()
        pltpu.make_async_copy(g.at[k], g.at[k], g_sems.at[k]).wait()
        total[...] += jnp.dot(g[k], w[part, :], preferred_element_type=F32)

    if stage == 2:
        for k in range(3):
            part = slice(k * 64, k * 64 + 64)
            tiles = swap_middle([total[part, t * 128 : t * 128 + 128] for t in range(6)])
            for t, v in enumerate(tiles):
                out[part, t * 128 : t * 128 + 128] = v.astype(out.dtype)
    elif sending:
        out[0:192, :] = total[192:384].astype(BF16)
        out[192:384, :] = total[0:192].astype(BF16)
    else:
        out[...] = total[...]


def product(stage, sending, stacks, pieces):
    rows, width = (384, 384) if stage == 1 else (192, 768)
    return pl.pallas_call(
        functools.partial(product_kernel, stage, sending),
        out_shape=jax.ShapeDtypeStruct((rows, width), BF16 if sending else F32),
        in_specs=[ANY] * 16,
        out_specs=VMEM,
        scratch_shapes=[
            pltpu.VMEM((3072, width), BF16),
            pltpu.VMEM((4, rows, 768), BF16),
            pltpu.VMEM((rows, width), F32),
            pltpu.SemaphoreType.DMA((4,)),
            pltpu.SemaphoreType.DMA((4,)),
        ],
        compiler_params=pltpu.CompilerParams(vmem_limit_bytes=16 << 20),
        cost_estimate=pl.CostEstimate(
            flops=384 * 768 * 3072, bytes_accessed=5 * 10**6, transcendentals=0
        ),
    )(*stacks, *pieces)


def right_operand(piece):
    mine = ring(piece, "zh")
    return mine + [shift(v, core=1) for v in mine]


def ladder_kernel(pair_list, pair_amps, ladder_ints, out):
    row = lax.broadcasted_iota(jnp.int32, (16, 64), 0)
    column = lax.broadcasted_iota(jnp.int32, (16, 64), 1)
    wanted = jnp.zeros((16, 64), jnp.int32)
    for i in range(16):
        wanted = jnp.where(row == i, pair_list[i], wanted)
    selector = jnp.where(wanted == column, 1.0, 0.0).astype(BF16)
    chosen = jnp.dot(selector, pair_amps[...], preferred_element_type=F32).astype(BF16)
    sums = jnp.dot(chosen, ladder_ints[...], preferred_element_type=F32)
    for c in range(32):
        out[c] = sums[:, c * 32 : c * 32 + 32]


def ladder_part(pair_amps, ladder_ints, pair_list):
    return pl.pallas_call(
        ladder_kernel,
        name="ladder",
        out_shape=jax.ShapeDtypeStruct((32, 16, 32), F32),
        in_specs=[SMEM, VMEM, VMEM],
        out_specs=VMEM,
        cost_estimate=pl.CostEstimate(
            flops=25 * 10**6, bytes_accessed=2 * 10**6, transcendentals=0
        ),
    )(pair_list, pair_amps, ladder_ints)


def on_device(
    tile_amps, cycle_ints, base_ints, amp_mask, int_mask, pair_amps, ladder_ints, pair_list
):
    va1, va2, base, keep, send_a, send_b = prepare(
        cycle_ints.T, tile_amps.T, base_ints.T, int_mask.T, amp_mask.T
    )
    came = shift(send_a, zl=1)
    x_blocks, y_blocks = ring(va1, "x"), ring(va2, "y")
    right = right_operand(jnp.concatenate([keep, came], axis=0))
    ints1, amps1 = stack(x_blocks)
    ints2, amps2 = stack(y_blocks)
    stacks = ring(ints1, "y") + ring(ints2, "x")
    send = product(1, True, stacks, right)
    came = shift(send, zl=1)
    keep = product(1, False, stacks, right)
    base = jnp.concatenate([base, shift(send_b, zl=1)], axis=0)

    parts = ladder_part(pair_amps, ladder_ints, pair_list)
    mine = lax.all_to_all(parts, "col", 0, 0)
    mine = mine.sum(axis=0)
    high = lax.reduce_precision(mine, 8, 7)
    rows = jnp.concatenate([high, mine - high], axis=1).astype(BF16)
    rows = jnp.pad(rows, ((0, 0), (0, 320)))

    stacks = ring(amps1, "y") + ring(amps2, "x")
    piece = base.astype(F32) + (keep + came.astype(F32))
    right = right_operand(jnp.concatenate([piece.astype(BF16), rows], axis=0))
    send = product(2, True, stacks, right)
    came = shift(send, zl=1)
    mine = [v[384:400, 0:64].astype(F32) for v in right]
    mine = functools.reduce(jnp.add, mine)
    ladder = mine[:, 0:32] + mine[:, 32:64]
    keep = product(2, False, stacks, right)
    return (keep + came.astype(F32)).T, ladder


def solution(mesh):
    in_specs = (
        P("row", "col"),
        P("row", "col"),
        P("row", "col"),
        P("row", "col"),
        P("row", "col"),
        P(None, ("row", "col")),
        P(("row", "col"), None),
        P(),
    )
    out_specs = (P("row", "col"), P(None, "col"))
    return jax.shard_map(
        on_device, mesh=mesh, in_specs=in_specs, out_specs=out_specs, check_vma=False
    )
```

time: 535 us -> 168 us (0.31)
  waiting for transfers between devices: 498 us -> 26.6 us
  starting transfers between devices: 0.2 us -> 78.9 us
  blocking collectives: 0 us -> 20.9 us
  Pallas kernels: 0 us -> 17.8 us
  matrix products: 15.4 us -> 0 us
  between operations: 15.3 us -> 0.84 us
  local copies, waits for them, and re-layouts: 2.65 us -> 16.4 us
    all_gather x4 -> x0, waiting for transfers between devices: 396 us -> none  [the longest x1 214 us: on_device(): lax.all_gather(integrals, 'col', axis=1, tiled=True)]
    psum x1 -> x0, waiting for transfers between devices: 101 us -> none  [on_device(): totals = lax.psum(partial_sums, ('row', 'col'))]
    ppermute x0 -> x36, starting transfers between devices: none -> 78.9 us  [shift(): return lax.ppermute(value, ('row', 'col'), pairs)]
    ppermute x0 -> x36, waiting for transfers between devices: none -> 26.6 us  [shift(): return lax.ppermute(value, ('row', 'col'), pairs)]
    all_to_all x0 -> x1, blocking collectives: none -> 20.9 us  [on_device(): mine = lax.all_to_all(parts, 'col', 0, 0)]
    pallas_call x0 -> x8, Pallas kernels: none -> 17.8 us  [the longest x4 12.3 us: product(): pl.pallas_call(functools.partial(product_kernel, stage, sending), out_sha...]
    unnamed x12 -> x41, local copies, waits for them, and re-layouts: 0.04 us -> 15.8 us
    dot_general x3 -> x0, matrix products: 15.4 us -> none  [the longest x1 7.21 us: on_device(): jnp.dot(lax.all_gather(amplitudes, 'col', axis=1, tiled=True), section, p...]
  transfers between devices with their start and end apart: 5 -> 36, of which waited for: 5 -> 9; matrix products, arithmetic and copies ran while one was open for 2% -> 5% of each run, Pallas kernels for 0% -> 7%
where the time goes in v1:
time: 168 us; the launch traced here: 167 us
  starting transfers between devices  78.9 us (47%)
  waiting for transfers between devices  26.6 us (16%)
  blocking collectives  20.9 us (12%)
  Pallas kernels  17.8 us (11%)
  local copies, waits for them, and re-layouts  16.4 us (10%)
  other arithmetic  5.07 us (3%)
    ppermute x36, starting transfers between devices, shift(): return lax.ppermute(value, ('row', 'col'), pairs)  78.9 us
    ppermute x36, waiting for transfers between devices, shift(): return lax.ppermute(value, ('row', 'col'), pairs)  26.6 us
    all_to_all x1, blocking collectives, on_device(): mine = lax.all_to_all(parts, 'col', 0, 0)  20.9 us
    unnamed x41, local copies, waits for them, and re-layouts  15.8 us
    pallas_call x4, Pallas kernels, product(): pl.pallas_call(functools.partial(product_kernel, stage, sending), out_sha...  12.3 us
  transfers between devices with their start and end apart: 36, of which 9 were waited for; matrix products, arithmetic and copies ran while one was open for 5% of the time, Pallas kernels for 7%

profile of v1, /device:TPU:1, one launch (start us, length us, event | category | flops | bytes accessed | tf_op | source)
XLA Modules:
  0.0 166.6 jit_solution(4170811149769882352)
XLA Ops:
  0.6 2.4 %prepare.1 = (bf16[4,96,384]{2,1,0:T(8,128)(2,1)}, bf16[4,96,384]{2,1,0:T(8,128)(2,1)}, bf16[192,384]{1,0:T(8,128)(2,1)}, bf16[192,384]{1,0:T(8,128)(2,1)}, bf16...) custom-call(bf16[192,768]{1,0:T(8,128)(2,1)} %bitcast.7, bf16[192,768]{1,0:T(8,128)(2,1)} %bitcast.8, ...), custom_call_target="tpu_custom_call" | custom-call | flops 1000000 | bytes 2000000 | tf_op jit(solution)/shard_map/prepare/pallas_call | solution.py:93
  3.0 2.5 %collective-permute-start.19 = (bf16[192,384]{1,0:T(8,128)(2,1)}, bf16[192,384]{1,0:T(8,128)(2,1)S(1)}, u32[]{:S(2)}, u32[]{:S(2)}) collective-permute-start(bf16[192,384]{1,0:T(8,128)(2,1)} %get-tuple-element.21), channel_id=1, source_target_pairs={{0,1},{1,0},{2,3},{3,2},{4,5},{5,4},{6,7},{7,6},{8,9},{9,8},{10,11... | collective-permute-start | bytes 442376 | tf_op jit(solution)/shard_map/ppermute | solution.py:23
  14.7 2.7 %collective-permute-start.2 = (bf16[4,96,384]{2,1,0:T(8,128)(2,1)}, bf16[4,96,384]{2,1,0:T(8,128)(2,1)S(1)}, u32[]{:S(2)}, u32[]{:S(2)}) collective-permute-start(bf16[4,96,384]{2,1,0:T(8,128)(2,1)} %get-tuple-element.12.a), channel_id=1, source_target_pairs={{0,4},{1,5},{2,6},{3,7},{4,0},{5,1},{6,2},{7,3},{8,12},{9,13},{10,... | collective-permute-start | bytes 884744 | tf_op jit(solution)/shard_map/ppermute | solution.py:23
  17.5 3.1 %collective-permute-start.20 = (bf16[384,384]{1,0:T(8,128)(2,1)S(1)}, bf16[384,384]{1,0:T(8,128)(2,1)S(1)}, u32[]{:S(2)}, u32[]{:S(2)}) collective-permute-start(bf16[384,384]{1,0:T(8,128)(2,1)S(1)} %constant_dynamic-update-slice_fusion.refs_8_), channel_id=1, source_target_pairs={{0,64},{1,65},{2,66},{3,67},{4,68},{5,69},{6,70},{7,71},{8,72},{9,... | collective-permute-start | bytes 884744 | tf_op jit(solution)/shard_map/ppermute | solution.py:23
  22.1 5.1 %collective-permute-start.21 = (bf16[384,384]{1,0:T(8,128)(2,1)S(1)}, bf16[384,384]{1,0:T(8,128)(2,1)S(1)}, u32[]{:S(2)}, u32[]{:S(2)}) collective-permute-start(bf16[384,384]{1,0:T(8,128)(2,1)S(1)} %constant_dynamic-update-slice_fusion.refs_8_), channel_id=1, source_target_pairs={{0,192},{1,193},{2,194},{3,195},{4,196},{5,197},{6,198},{7,199},{8... | collective-permute-start | bytes 884744 | tf_op jit(solution)/shard_map/ppermute | solution.py:23
  30.9 2.7 %collective-permute-start.23 = (bf16[384,384]{1,0:T(8,128)(2,1)S(1)}, bf16[384,384]{1,0:T(8,128)(2,1)S(1)}, u32[]{:S(2)}, u32[]{:S(2)}) collective-permute-start(bf16[384,384]{1,0:T(8,128)(2,1)S(1)} %constant_dynamic-update-slice_fusion.refs_8_), channel_id=1, source_target_pairs={{0,32},{1,33},{2,34},{3,35},{4,36},{5,37},{6,38},{7,39},{8,40},{9,... | collective-permute-start | bytes 884744 | tf_op jit(solution)/shard_map/ppermute | solution.py:23
  33.6 3.1 %collective-permute-start.24 = (bf16[384,384]{1,0:T(8,128)(2,1)S(1)}, bf16[384,384]{1,0:T(8,128)(2,1)S(1)}, u32[]{:S(2)}, u32[]{:S(2)}) collective-permute-start(bf16[384,384]{1,0:T(8,128)(2,1)S(1)} %collective-permute-done.20.refs_9_), channel_id=1, source_target_pairs={{0,32},{1,33},{2,34},{3,35},{4,36},{5,37},{6,38},{7,39},{8,40},{9,... | collective-permute-start | bytes 884744 | tf_op jit(solution)/shard_map/ppermute | solution.py:23
  36.7 10.5 %collective-permute-done.21.refs_10_ = bf16[384,384]{1,0:T(8,128)(2,1)S(1)} collective-permute-done((bf16[384,384]{1,0:T(8,128)(2,1)S(1)}, bf16[384,384]{1,0:T(8,128)(2,1)S(1)}, u32[]{:S(2)}, u32[]{:S(2)}) %collective-permute-start.21) | collective-permute-done | bytes 294944 | tf_op jit(solution)/shard_map/ppermute | solution.py:23
  48.7 3.6 %collective-permute-start.17 = (bf16[4,2,96,384]{3,2,1,0:T(8,128)(2,1)S(1)}, bf16[4,2,96,384]{3,2,1,0:T(8,128)(2,1)S(1)}, u32[]{:S(2)}, u32[]{:S(2)}) collective-permute-start(bf16[4,2,96,384]{3,2,1,0:T(8,128)(2,1)S(1)} %get-tuple-element.19.refs_4_), channel_id=1, source_target_pairs={{0,6},{1,7},{2,0},{3,1},{4,2},{5,3},{6,4},{7,5},{8,14},{9,15},{10,... | collective-permute-start | bytes 1769480 | tf_op jit(solution)/shard_map/ppermute | solution.py:23
  59.4 2.7 %ladder.1 = f32[32,16,32]{2,1,0:T(8,128)} custom-call(s32[16]{0:T(128)} %pair_list.1, bf16[64,768]{1,0:T(8,128)(2,1)} %pair_amps.1, bf16[768,1024]{1,0:T(8,128)(2,1)} %ladder_ints.1), custom_call_target="tpu_custom_call" | custom-call | flops 25000000 | bytes 2000000 | tf_op jit(solution)/shard_map/ladder/pallas_call | solution.py:232
  63.8 20.9 %all_to_all.5 = f32[32,1,512]{2,1,0:T(1,128)} all-to-all(f32[32,1,512]{2,1,0:T(1,128)} %reshape.4), channel_id=1, replica_groups=mesh['row'=8,'col'=32] {'col'}, dimensions={0} | all-to-all | bytes 131072 | tf_op jit(solution)/shard_map/all_to_all | solution.py:262
  85.2 2.3 %reduce = f32[32,512]{1,0:T(8,128)} reduce(f32[32,1,512]{2,1,0:T(1,128)} %all_to_all.5, f32[]{:T(128)} %broadcast.6), dimensions={1}, to_apply=%all_to_all.3.reduce_sub_computation | reduce | bytes 131076 | tf_op jit(solution)/shard_map/all_to_all | solution.py:262
  90.1 6.5 %collective-permute-start.12 = (bf16[192,384]{1,0:T(8,128)(2,1)}, bf16[192,384]{1,0:T(8,128)(2,1)S(1)}, u32[]{:S(2)}, u32[]{:S(2)}) collective-permute-start(bf16[192,384]{1,0:T(8,128)(2,1)} %get-tuple-element.17), channel_id=1, source_target_pairs={{0,1},{1,0},{2,3},{3,2},{4,5},{5,4},{6,7},{7,6},{8,9},{9,8},{10,11... | collective-permute-start | bytes 442376 | tf_op jit(solution)/shard_map/ppermute | solution.py:23
  107.6 3.0 %shard_map.96 = bf16[384,384]{1,0:T(8,128)(2,1)S(1)} custom-call(bf16[4,2,96,384]{3,2,1,0:T(8,128)(2,1)S(1)} %get-tuple-element.18.refs_0_, bf16[4,2,96,384]{3,2,1,0:T(8,128)(2,1)} %collective-permute-done.13.refs_1_, bf16[4,2,96,384]{3,2,1,0:T(8,128)(2,1)} %collective-permute-done.14.refs_2_, bf16[4,2,96,384]{3,2,1,0:T(8,128)(2,1)} %collective-permute-done.15.refs_3_, ...), custom_call_target="tpu_custom_call" | custom-call | flops 905969664 | bytes 5000000 | tf_op jit(solution)/shard_map/pallas_call | solution.py:194
  111.4 3.0 %shard_map.95 = f32[384,384]{1,0:T(8,128)S(1)} custom-call(bf16[4,2,96,384]{3,2,1,0:T(8,128)(2,1)S(1)} %get-tuple-element.18.refs_0_, bf16[4,2,96,384]{3,2,1,0:T(8,128)(2,1)} %collective-permute-done.13.refs_1_, bf16[4,2,96,384]{3,2,1,0:T(8,128)(2,1)} %collective-permute-done.14.refs_2_, bf16[4,2,96,384]{3,2,1,0:T(8,128)(2,1)} %collective-permute-done.15.refs_3_, ...), custom_call_target="tpu_custom_call" | custom-call | flops 905969664 | bytes 5000000 | tf_op jit(solution)/shard_map/pallas_call | solution.py:194
  114.4 3.1 %collective-permute-done.27 = bf16[384,384]{1,0:T(8,128)(2,1)S(1)} collective-permute-done((bf16[384,384]{1,0:T(8,128)(2,1)S(1)}, bf16[384,384]{1,0:T(8,128)(2,1)S(1)}, u32[]{:S(2)}, u32[]{:S(2)}) %collective-permute-start.27) | collective-permute-done | bytes 294944 | tf_op jit(solution)/shard_map/ppermute | solution.py:23
  118.5 3.6 %collective-permute-start.29 = (bf16[400,384]{1,0:T(8,128)(2,1)S(1)}, bf16[400,384]{1,0:T(8,128)(2,1)S(1)}, u32[]{:S(2)}, u32[]{:S(2)}) collective-permute-start(bf16[400,384]{1,0:T(8,128)(2,1)S(1)} %fusion.1.refs_8_), channel_id=1, source_target_pairs={{0,192},{1,193},{2,194},{3,195},{4,196},{5,197},{6,198},{7,199},{8... | collective-permute-start | bytes 921608 | tf_op jit(solution)/shard_map/ppermute | solution.py:23
  122.0 4.8 %collective-permute-done.9.refs_5_ = bf16[4,2,96,384]{3,2,1,0:T(8,128)(2,1)S(1)} collective-permute-done((bf16[4,2,96,384]{3,2,1,0:T(8,128)(2,1)S(1)}, bf16[4,2,96,384]{3,2,1,0:T(8,128)(2,1)S(1)}, u32[]{:S(2)}, u32[]{:S(2)}) %collective-permute-start.9) | collective-permute-done | bytes 589856 | tf_op jit(solution)/shard_map/ppermute | solution.py:23
  126.9 4.1 %collective-permute-start.30 = (bf16[400,384]{1,0:T(8,128)(2,1)S(1)}, bf16[400,384]{1,0:T(8,128)(2,1)S(1)}, u32[]{:S(2)}, u32[]{:S(2)}) collective-permute-start(bf16[400,384]{1,0:T(8,128)(2,1)S(1)} %fusion.1.refs_8_), channel_id=1, source_target_pairs={{0,128},{1,129},{2,130},{3,131},{4,132},{5,133},{6,134},{7,135},{8... | collective-permute-start | bytes 921608 | tf_op jit(solution)/shard_map/ppermute | solution.py:23
  133.2 9.9 %collective-permute-start.32 = (bf16[400,384]{1,0:T(8,128)(2,1)S(1)}, bf16[400,384]{1,0:T(8,128)(2,1)S(1)}, u32[]{:S(2)}, u32[]{:S(2)}) collective-permute-start(bf16[400,384]{1,0:T(8,128)(2,1)S(1)} %collective-permute-done.28.refs_9_), channel_id=1, source_target_pairs={{0,32},{1,33},{2,34},{3,35},{4,36},{5,37},{6,38},{7,39},{8,40},{9,... | collective-permute-start | bytes 921608 | tf_op jit(solution)/shard_map/ppermute | solution.py:23
  146.9 3.1 %shard_map.98 = bf16[192,768]{1,0:T(8,128)(2,1)S(1)} custom-call(bf16[4,2,96,384]{3,2,1,0:T(8,128)(2,1)S(1)} %get-tuple-element.13.refs_0_, bf16[4,2,96,384]{3,2,1,0:T(8,128)(2,1)S(1)} %collective-permute-done.3.refs_1_, bf16[4,2,96,384]{3,2,1,0:T(8,128)(2,1)S(1)} %collective-permute-done.4.refs_2_, ...), custom_call_target="tpu_custom_call" | custom-call | flops 905969664 | bytes 5000000 | tf_op jit(solution)/shard_map/pallas_call | solution.py:194
  150.0 8.7 %collective-permute-start.35 = (bf16[192,768]{1,0:T(8,128)(2,1)S(1)}, bf16[192,768]{1,0:T(8,128)(2,1)S(1)}, u32[]{:S(2)}, u32[]{:S(2)}) collective-permute-start(bf16[192,768]{1,0:T(8,128)(2,1)S(1)} %shard_map.98), channel_id=1, source_target_pairs={{0,1},{1,0},{2,3},{3,2},{4,5},{5,4},{6,7},{7,6},{8,9},{9,8},{10,11... | collective-permute-start | bytes 884744 | tf_op jit(solution)/shard_map/ppermute | solution.py:23
  158.8 3.2 %shard_map.97 = f32[192,768]{1,0:T(8,128)S(1)} custom-call(bf16[4,2,96,384]{3,2,1,0:T(8,128)(2,1)S(1)} %get-tuple-element.13.refs_0_, bf16[4,2,96,384]{3,2,1,0:T(8,128)(2,1)S(1)} %collective-permute-done.3.refs_1_, bf16[4,2,96,384]{3,2,1,0:T(8,128)(2,1)S(1)} %collective-permute-done.4.refs_2_, bf16[4,2,96,384]{3,2,1,0:T(8,128)(2,1)S(1)} %collective-permute-done.5.refs_3_, ...), custom_call_target="tpu_custom_call" | custom-call | flops 905969664 | bytes 5000000 | tf_op jit(solution)/shard_map/pallas_call | solution.py:194
  162.7 3.1 %collective-permute-done.35 = bf16[192,768]{1,0:T(8,128)(2,1)S(1)} collective-permute-done((bf16[192,768]{1,0:T(8,128)(2,1)S(1)}, bf16[192,768]{1,0:T(8,128)(2,1)S(1)}, u32[]{:S(2)}, u32[]{:S(2)}) %collective-permute-start.35) | collective-permute-done | bytes 294944 | tf_op jit(solution)/shard_map/ppermute | solution.py:23
  (109 shorter events, 48.2 us)
Async XLA Ops:
  9.9 17.3 %collective-permute-start = (bf16[4,96,384]{2,1,0:T(8,128)(2,1)}, bf16[4,96,384]{2,1,0:T(8,128)(2,1)S(1)}, u32[]{:S(2)}, u32[]{:S(2)}) collective-permute-start(bf16[4,96,384]{2,1,0:T(8,128)(2,1)} %get-tuple-element.12.a), channel_id=1, source_target_pairs={{0,2},{1,3},{2,4},{3,5},{4,6},{5,7},{6,0},{7,1},{8,10},{9,11},{10,... | collective-permute-start | bytes 884744 | tf_op jit(solution)/shard_map/ppermute | solution.py:23
  11.2 18.5 %collective-permute-start.1 = (bf16[4,96,384]{2,1,0:T(8,128)(2,1)}, bf16[4,96,384]{2,1,0:T(8,128)(2,1)S(1)}, u32[]{:S(2)}, u32[]{:S(2)}) collective-permute-start(bf16[4,96,384]{2,1,0:T(8,128)(2,1)} %get-tuple-element.12.a), channel_id=1, source_target_pairs={{0,6},{1,7},{2,0},{3,1},{4,2},{5,3},{6,4},{7,5},{8,14},{9,15},{10,... | collective-permute-start | bytes 884744 | tf_op jit(solution)/shard_map/ppermute | solution.py:23
  14.7 16.2 %collective-permute-start.2 = (bf16[4,96,384]{2,1,0:T(8,128)(2,1)}, bf16[4,96,384]{2,1,0:T(8,128)(2,1)S(1)}, u32[]{:S(2)}, u32[]{:S(2)}) collective-permute-start(bf16[4,96,384]{2,1,0:T(8,128)(2,1)} %get-tuple-element.12.a), channel_id=1, source_target_pairs={{0,4},{1,5},{2,6},{3,7},{4,0},{5,1},{6,2},{7,3},{8,12},{9,13},{10,... | collective-permute-start | bytes 884744 | tf_op jit(solution)/shard_map/ppermute | solution.py:23
  17.5 16.1 %collective-permute-start.20 = (bf16[384,384]{1,0:T(8,128)(2,1)S(1)}, bf16[384,384]{1,0:T(8,128)(2,1)S(1)}, u32[]{:S(2)}, u32[]{:S(2)}) collective-permute-start(bf16[384,384]{1,0:T(8,128)(2,1)S(1)} %constant_dynamic-update-slice_fusion.refs_8_), channel_id=1, source_target_pairs={{0,64},{1,65},{2,66},{3,67},{4,68},{5,69},{6,70},{7,71},{8,72},{9,... | collective-permute-start | bytes 884744 | tf_op jit(solution)/shard_map/ppermute | solution.py:23
  22.1 25.1 %collective-permute-start.21 = (bf16[384,384]{1,0:T(8,128)(2,1)S(1)}, bf16[384,384]{1,0:T(8,128)(2,1)S(1)}, u32[]{:S(2)}, u32[]{:S(2)}) collective-permute-start(bf16[384,384]{1,0:T(8,128)(2,1)S(1)} %constant_dynamic-update-slice_fusion.refs_8_), channel_id=1, source_target_pairs={{0,192},{1,193},{2,194},{3,195},{4,196},{5,197},{6,198},{7,199},{8... | collective-permute-start | bytes 884744 | tf_op jit(solution)/shard_map/ppermute | solution.py:23
  27.3 20.6 %collective-permute-start.22 = (bf16[384,384]{1,0:T(8,128)(2,1)S(1)}, bf16[384,384]{1,0:T(8,128)(2,1)S(1)}, u32[]{:S(2)}, u32[]{:S(2)}) collective-permute-start(bf16[384,384]{1,0:T(8,128)(2,1)S(1)} %constant_dynamic-update-slice_fusion.refs_8_), channel_id=1, source_target_pairs={{0,128},{1,129},{2,130},{3,131},{4,132},{5,133},{6,134},{7,135},{8... | collective-permute-start | bytes 884744 | tf_op jit(solution)/shard_map/ppermute | solution.py:23
  29.7 28.7 %collective-permute-start.16 = (bf16[4,2,96,384]{3,2,1,0:T(8,128)(2,1)S(1)}, bf16[4,2,96,384]{3,2,1,0:T(8,128)(2,1)S(1)}, u32[]{:S(2)}, u32[]{:S(2)}) collective-permute-start(bf16[4,2,96,384]{3,2,1,0:T(8,128)(2,1)S(1)} %get-tuple-element.19.refs_4_), channel_id=1, source_target_pairs={{0,2},{1,3},{2,4},{3,5},{4,6},{5,7},{6,0},{7,1},{8,10},{9,11},{10,... | collective-permute-start | bytes 1769480 | tf_op jit(solution)/shard_map/ppermute | solution.py:23
  30.9 17.0 %collective-permute-start.23 = (bf16[384,384]{1,0:T(8,128)(2,1)S(1)}, bf16[384,384]{1,0:T(8,128)(2,1)S(1)}, u32[]{:S(2)}, u32[]{:S(2)}) collective-permute-start(bf16[384,384]{1,0:T(8,128)(2,1)S(1)} %constant_dynamic-update-slice_fusion.refs_8_), channel_id=1, source_target_pairs={{0,32},{1,33},{2,34},{3,35},{4,36},{5,37},{6,38},{7,39},{8,40},{9,... | collective-permute-start | bytes 884744 | tf_op jit(solution)/shard_map/ppermute | solution.py:23
  33.6 18.9 %collective-permute-start.24 = (bf16[384,384]{1,0:T(8,128)(2,1)S(1)}, bf16[384,384]{1,0:T(8,128)(2,1)S(1)}, u32[]{:S(2)}, u32[]{:S(2)}) collective-permute-start(bf16[384,384]{1,0:T(8,128)(2,1)S(1)} %collective-permute-done.20.refs_9_), channel_id=1, source_target_pairs={{0,32},{1,33},{2,34},{3,35},{4,36},{5,37},{6,38},{7,39},{8,40},{9,... | collective-permute-start | bytes 884744 | tf_op jit(solution)/shard_map/ppermute | solution.py:23
  48.7 41.4 %collective-permute-start.17 = (bf16[4,2,96,384]{3,2,1,0:T(8,128)(2,1)S(1)}, bf16[4,2,96,384]{3,2,1,0:T(8,128)(2,1)S(1)}, u32[]{:S(2)}, u32[]{:S(2)}) collective-permute-start(bf16[4,2,96,384]{3,2,1,0:T(8,128)(2,1)S(1)} %get-tuple-element.19.refs_4_), channel_id=1, source_target_pairs={{0,6},{1,7},{2,0},{3,1},{4,2},{5,3},{6,4},{7,5},{8,14},{9,15},{10,... | collective-permute-start | bytes 1769480 | tf_op jit(solution)/shard_map/ppermute | solution.py:23
  53.3 43.3 %collective-permute-start.18 = (bf16[4,2,96,384]{3,2,1,0:T(8,128)(2,1)S(1)}, bf16[4,2,96,384]{3,2,1,0:T(8,128)(2,1)}, u32[]{:S(2)}, u32[]{:S(2)}) collective-permute-start(bf16[4,2,96,384]{3,2,1,0:T(8,128)(2,1)S(1)} %get-tuple-element.19.refs_4_), channel_id=1, source_target_pairs={{0,4},{1,5},{2,6},{3,7},{4,0},{5,1},{6,2},{7,3},{8,12},{9,13},{10,... | collective-permute-start | bytes 1769480 | tf_op jit(solution)/shard_map/ppermute | solution.py:23
  55.0 42.5 %collective-permute-start.13 = (bf16[4,2,96,384]{3,2,1,0:T(8,128)(2,1)S(1)}, bf16[4,2,96,384]{3,2,1,0:T(8,128)(2,1)}, u32[]{:S(2)}, u32[]{:S(2)}) collective-permute-start(bf16[4,2,96,384]{3,2,1,0:T(8,128)(2,1)S(1)} %get-tuple-element.18.refs_0_), channel_id=1, source_target_pairs={{0,8},{1,9},{2,10},{3,11},{4,12},{5,13},{6,14},{7,15},{8,16},{9,17... | collective-permute-start | bytes 1769480 | tf_op jit(solution)/shard_map/ppermute | solution.py:23
  56.3 42.8 %collective-permute-start.14 = (bf16[4,2,96,384]{3,2,1,0:T(8,128)(2,1)S(1)}, bf16[4,2,96,384]{3,2,1,0:T(8,128)(2,1)}, u32[]{:S(2)}, u32[]{:S(2)}) collective-permute-start(bf16[4,2,96,384]{3,2,1,0:T(8,128)(2,1)S(1)} %get-tuple-element.18.refs_0_), channel_id=1, source_target_pairs={{0,24},{1,25},{2,26},{3,27},{4,28},{5,29},{6,30},{7,31},{8,0},{9,1... | collective-permute-start | bytes 1769480 | tf_op jit(solution)/shard_map/ppermute | solution.py:23
  58.4 41.5 %collective-permute-start.15 = (bf16[4,2,96,384]{3,2,1,0:T(8,128)(2,1)S(1)}, bf16[4,2,96,384]{3,2,1,0:T(8,128)(2,1)}, u32[]{:S(2)}, u32[]{:S(2)}) collective-permute-start(bf16[4,2,96,384]{3,2,1,0:T(8,128)(2,1)S(1)} %get-tuple-element.18.refs_0_), channel_id=1, source_target_pairs={{0,16},{1,17},{2,18},{3,19},{4,20},{5,21},{6,22},{7,23},{8,24},{9,... | collective-permute-start | bytes 1769480 | tf_op jit(solution)/shard_map/ppermute | solution.py:23
  90.1 20.7 %collective-permute-start.12 = (bf16[192,384]{1,0:T(8,128)(2,1)}, bf16[192,384]{1,0:T(8,128)(2,1)S(1)}, u32[]{:S(2)}, u32[]{:S(2)}) collective-permute-start(bf16[192,384]{1,0:T(8,128)(2,1)} %get-tuple-element.17), channel_id=1, source_target_pairs={{0,1},{1,0},{2,3},{3,2},{4,5},{5,4},{6,7},{7,6},{8,9},{9,8},{10,11... | collective-permute-start | bytes 442376 | tf_op jit(solution)/shard_map/ppermute | solution.py:23
  96.6 21.8 %collective-permute-start.10 = (bf16[4,2,96,384]{3,2,1,0:T(8,128)(2,1)S(1)}, bf16[4,2,96,384]{3,2,1,0:T(8,128)(2,1)S(1)}, u32[]{:S(2)}, u32[]{:S(2)}) collective-permute-start(bf16[4,2,96,384]{3,2,1,0:T(8,128)(2,1)S(1)} %get-tuple-element.15.refs_4_), channel_id=1, source_target_pairs={{0,6},{1,7},{2,0},{3,1},{4,2},{5,3},{6,4},{7,5},{8,14},{9,15},{10,... | collective-permute-start | bytes 1769480 | tf_op jit(solution)/shard_map/ppermute | solution.py:23
  97.5 21.0 %collective-permute-start.11 = (bf16[4,2,96,384]{3,2,1,0:T(8,128)(2,1)S(1)}, bf16[4,2,96,384]{3,2,1,0:T(8,128)(2,1)S(1)}, u32[]{:S(2)}, u32[]{:S(2)}) collective-permute-start(bf16[4,2,96,384]{3,2,1,0:T(8,128)(2,1)S(1)} %get-tuple-element.15.refs_4_), channel_id=1, source_target_pairs={{0,4},{1,5},{2,6},{3,7},{4,0},{5,1},{6,2},{7,3},{8,12},{9,13},{10,... | collective-permute-start | bytes 1769480 | tf_op jit(solution)/shard_map/ppermute | solution.py:23
  99.1 27.7 %collective-permute-start.9 = (bf16[4,2,96,384]{3,2,1,0:T(8,128)(2,1)S(1)}, bf16[4,2,96,384]{3,2,1,0:T(8,128)(2,1)S(1)}, u32[]{:S(2)}, u32[]{:S(2)}) collective-permute-start(bf16[4,2,96,384]{3,2,1,0:T(8,128)(2,1)S(1)} %get-tuple-element.15.refs_4_), channel_id=1, source_target_pairs={{0,2},{1,3},{2,4},{3,5},{4,6},{5,7},{6,0},{7,1},{8,10},{9,11},{10,... | collective-permute-start | bytes 1769480 | tf_op jit(solution)/shard_map/ppermute | solution.py:23
  110.8 20.2 %collective-permute-start.3 = (bf16[4,2,96,384]{3,2,1,0:T(8,128)(2,1)S(1)}, bf16[4,2,96,384]{3,2,1,0:T(8,128)(2,1)S(1)}, u32[]{:S(2)}, u32[]{:S(2)}) collective-permute-start(bf16[4,2,96,384]{3,2,1,0:T(8,128)(2,1)S(1)} %get-tuple-element.13.refs_0_), channel_id=1, source_target_pairs={{0,8},{1,9},{2,10},{3,11},{4,12},{5,13},{6,14},{7,15},{8,16},{9,17... | collective-permute-start | bytes 1769480 | tf_op jit(solution)/shard_map/ppermute | solution.py:23
  118.4 14.9 %collective-permute-start.28 = (bf16[400,384]{1,0:T(8,128)(2,1)S(1)}, bf16[400,384]{1,0:T(8,128)(2,1)S(1)}, u32[]{:S(2)}, u32[]{:S(2)}) collective-permute-start(bf16[400,384]{1,0:T(8,128)(2,1)S(1)} %fusion.1.refs_8_), channel_id=1, source_target_pairs={{0,64},{1,65},{2,66},{3,67},{4,68},{5,69},{6,70},{7,71},{8,72},{9,... | collective-permute-start | bytes 921608 | tf_op jit(solution)/shard_map/ppermute | solution.py:23
  118.5 24.6 %collective-permute-start.29 = (bf16[400,384]{1,0:T(8,128)(2,1)S(1)}, bf16[400,384]{1,0:T(8,128)(2,1)S(1)}, u32[]{:S(2)}, u32[]{:S(2)}) collective-permute-start(bf16[400,384]{1,0:T(8,128)(2,1)S(1)} %fusion.1.refs_8_), channel_id=1, source_target_pairs={{0,192},{1,193},{2,194},{3,195},{4,196},{5,197},{6,198},{7,199},{8... | collective-permute-start | bytes 921608 | tf_op jit(solution)/shard_map/ppermute | solution.py:23
  126.9 17.4 %collective-permute-start.30 = (bf16[400,384]{1,0:T(8,128)(2,1)S(1)}, bf16[400,384]{1,0:T(8,128)(2,1)S(1)}, u32[]{:S(2)}, u32[]{:S(2)}) collective-permute-start(bf16[400,384]{1,0:T(8,128)(2,1)S(1)} %fusion.1.refs_8_), channel_id=1, source_target_pairs={{0,128},{1,129},{2,130},{3,131},{4,132},{5,133},{6,134},{7,135},{8... | collective-permute-start | bytes 921608 | tf_op jit(solution)/shard_map/ppermute | solution.py:23
  131.0 14.8 %collective-permute-start.5 = (bf16[4,2,96,384]{3,2,1,0:T(8,128)(2,1)S(1)}, bf16[4,2,96,384]{3,2,1,0:T(8,128)(2,1)S(1)}, u32[]{:S(2)}, u32[]{:S(2)}) collective-permute-start(bf16[4,2,96,384]{3,2,1,0:T(8,128)(2,1)S(1)} %get-tuple-element.13.refs_0_), channel_id=1, source_target_pairs={{0,16},{1,17},{2,18},{3,19},{4,20},{5,21},{6,22},{7,23},{8,24},{9,... | collective-permute-start | bytes 1769480 | tf_op jit(solution)/shard_map/ppermute | solution.py:23
  150.0 15.7 %collective-permute-start.35 = (bf16[192,768]{1,0:T(8,128)(2,1)S(1)}, bf16[192,768]{1,0:T(8,128)(2,1)S(1)}, u32[]{:S(2)}, u32[]{:S(2)}) collective-permute-start(bf16[192,768]{1,0:T(8,128)(2,1)S(1)} %shard_map.98), channel_id=1, source_target_pairs={{0,1},{1,0},{2,3},{3,2},{4,5},{5,4},{6,7},{7,6},{8,9},{9,8},{10,11... | collective-permute-start | bytes 884744 | tf_op jit(solution)/shard_map/ppermute | solution.py:23
  (31 other events, 254.2 us)

commit v2 on v1

--- a/solution.py
+++ b/solution.py
@@ -93,6 +93,7 @@
     return pl.pallas_call(
         prepare_kernel,
         name="prepare",
+        compiler_params=pltpu.CompilerParams(vmem_limit_bytes=65600000),
         out_shape=(
             struct((4, 96, 384), BF16),
             struct((4, 96, 384), BF16),
@@ -107,6 +108,32 @@
     )(vt, at, bt, int_mask, amp_mask)
 
 
+def join_kernel(a, b, out, sem):
+    copies = []
+    for i, ref in enumerate((a, b)):
+        for lane in (0, 128, 256):
+            lanes = pl.ds(lane, 128)
+            into = out.at[pl.ds(192 * i, 192), lanes]
+            copies.append(pltpu.make_async_copy(ref.at[:, lanes], into, sem))
+    for copy in copies:
+        copy.start()
+    for copy in copies:
+        copy.wait()
+
+
+def join(a, b):
+    return pl.pallas_call(
+        join_kernel,
+        name="join",
+        out_shape=jax.ShapeDtypeStruct((384, 384), BF16),
+        in_specs=[ANY] * 2,
+        out_specs=VMEM,
+        scratch_shapes=[pltpu.SemaphoreType.DMA],
+        compiler_params=pltpu.CompilerParams(vmem_limit_bytes=4 << 20),
+        cost_estimate=pl.CostEstimate(flops=1000, bytes_accessed=6 * 10**5, transcendentals=0),
+    )(a, b)
+
+
 def stack_kernel(a, b, c, d, ints, amps, sem):
     copies = []
     for i, ref in enumerate((a, b, c, d)):
@@ -140,7 +167,7 @@
 def product_kernel(stage, sending, *refs):
     stacks, pieces, (out, w, g, total, w_sems, g_sems) = refs[:8], refs[8:16], refs[16:]
     zh, core, y, x, _ = place()
-    rows = slice(None) if stage == 1 else slice(192, 384) if sending else slice(0, 192)
+    count = g.shape[1]
     sides = ((0 if sending else 1),) if stage == 1 else (0, 1)
 
     @pl.loop(0, 4)
@@ -163,7 +190,7 @@
         for other in range(2):
             at_z, at_core = lax.rem(zh + dz + 4, 4), lax.rem(core + other, 2)
             pltpu.make_async_copy(
-                pieces[other * 4 + i].at[rows if stage == 2 else slice(0, 384)],
+                pieces[other * 4 + i].at[pl.ds(0, count)],
                 g.at[at_z, :, pl.ds(pl.multiple_of(at_core * 384, 128), 384)],
                 g_sems.at[at_z],
             ).start()
@@ -225,20 +252,72 @@
     chosen = jnp.dot(selector, pair_amps[...], preferred_element_type=F32).astype(BF16)
     sums = jnp.dot(chosen, ladder_ints[...], preferred_element_type=F32)
     for c in range(32):
-        out[c] = sums[:, c * 32 : c * 32 + 32]
+        for j in range(4):
+            out[c, :, j * 32 : j * 32 + 32] = sums[j * 4 : j * 4 + 4, c * 32 : c * 32 + 32]
+
+
+def ladder_sum_kernel(parts, out):
+    total = jnp.concatenate([jnp.sum(parts[...], axis=0), jnp.zeros((12, 128), F32)], axis=0)
+    high = total.astype(BF16)
+    out[:, 0:128] = high
+    out[:, 128:256] = (total - high.astype(F32)).astype(BF16)
+    out[:, 256:384] = jnp.zeros((16, 128), BF16)
+
+
+def ladder_sum(parts):
+    return pl.pallas_call(
+        ladder_sum_kernel,
+        name="ladder_sum",
+        compiler_params=pltpu.CompilerParams(vmem_limit_bytes=1 << 20),
+        out_shape=jax.ShapeDtypeStruct((16, 384), BF16),
+        in_specs=[VMEM],
+        out_specs=VMEM,
+        cost_estimate=pl.CostEstimate(flops=20000, bytes_accessed=80000, transcendentals=0),
+    )(parts)
 
 
 def ladder_part(pair_amps, ladder_ints, pair_list):
     return pl.pallas_call(
         ladder_kernel,
         name="ladder",
-        out_shape=jax.ShapeDtypeStruct((32, 16, 32), F32),
+        compiler_params=pltpu.CompilerParams(vmem_limit_bytes=6 << 20),
+        out_shape=jax.ShapeDtypeStruct((32, 4, 128), F32),
         in_specs=[SMEM, VMEM, VMEM],
         out_specs=VMEM,
         cost_estimate=pl.CostEstimate(
             flops=25 * 10**6, bytes_accessed=2 * 10**6, transcendentals=0
         ),
     )(pair_list, pair_amps, ladder_ints)
+
+
+def ladder_end_kernel(*refs):
+    pieces, (out, rows, sem) = refs[:8], refs[8:]
+    copies = []
+    for i, ref in enumerate(pieces):
+        copies.append(pltpu.make_async_copy(ref.at[pl.ds(192, 16)], rows.at[i], sem))
+    for copy in copies:
+        copy.start()
+    for copy in copies:
+        copy.wait()
+    total = rows[0].astype(F32)
+    for i in range(1, 8):
+        total += rows[i].astype(F32)
+    total = total[0:4, 0:128] + total[0:4, 128:256]
+    for j in range(4):
+        out[j * 4 : j * 4 + 4, :] = total[:, j * 32 : j * 32 + 32]
+
+
+def ladder_end(pieces):
+    return pl.pallas_call(
+        ladder_end_kernel,
+        name="ladder_end",
+        out_shape=jax.ShapeDtypeStruct((16, 32), F32),
+        in_specs=[ANY] * 8,
+        out_specs=VMEM,
+        scratch_shapes=[pltpu.VMEM((8, 16, 384), BF16), pltpu.SemaphoreType.DMA],
+        compiler_params=pltpu.CompilerParams(vmem_limit_bytes=1 << 20),
+        cost_estimate=pl.CostEstimate(flops=20000, bytes_accessed=100000, transcendentals=0),
+    )(*pieces)
 
 
 def on_device(
@@ -249,7 +328,7 @@
     )
     came = shift(send_a, zl=1)
     x_blocks, y_blocks = ring(va1, "x"), ring(va2, "y")
-    right = right_operand(jnp.concatenate([keep, came], axis=0))
+    right = right_operand(join(keep, came))
     ints1, amps1 = stack(x_blocks)
     ints2, amps2 = stack(y_blocks)
     stacks = ring(ints1, "y") + ring(ints2, "x")
@@ -259,21 +338,18 @@
     base = jnp.concatenate([base, shift(send_b, zl=1)], axis=0)
 
     parts = ladder_part(pair_amps, ladder_ints, pair_list)
-    mine = lax.all_to_all(parts, "col", 0, 0)
-    mine = mine.sum(axis=0)
-    high = lax.reduce_precision(mine, 8, 7)
-    rows = jnp.concatenate([high, mine - high], axis=1).astype(BF16)
-    rows = jnp.pad(rows, ((0, 0), (0, 320)))
+    parts = lax.all_to_all(parts, "col", 0, 0)
+    rows = ladder_sum(parts)
 
     stacks = ring(amps1, "y") + ring(amps2, "x")
-    piece = base.astype(F32) + (keep + came.astype(F32))
-    right = right_operand(jnp.concatenate([piece.astype(BF16), rows], axis=0))
-    send = product(2, True, stacks, right)
+    piece = (base.astype(F32) + (keep + came.astype(F32))).astype(BF16)
+    away = right_operand(piece[192:])
+    mine = right_operand(jnp.concatenate([piece[:192], rows], axis=0))
+    send = product(2, True, stacks, away)
     came = shift(send, zl=1)
-    mine = [v[384:400, 0:64].astype(F32) for v in right]
-    mine = functools.reduce(jnp.add, mine)
-    ladder = mine[:, 0:32] + mine[:, 32:64]
-    keep = product(2, False, stacks, right)
+    keep = product(2, False, stacks, mine)
+    keep, *mine = lax.optimization_barrier((keep, *mine))
+    ladder = ladder_end(mine)
     return (keep + came.astype(F32)).T, ladder
 
 

time: 168 us -> 171 us (1.018)
  starting transfers between devices: 78.9 us -> 111 us
  blocking collectives: 20.9 us -> 0 us
  local copies, waits for them, and re-layouts: 16.4 us -> 3.27 us
  waiting for transfers between devices: 26.6 us -> 33.3 us
  other arithmetic: 5.07 us -> 1.9 us
    ppermute x36 -> x43, starting transfers between devices: 78.9 us -> 106 us  [shift(): return lax.ppermute(value, ('row', 'col'), pairs)]
    all_to_all x1 -> x0, blocking collectives: 20.9 us -> none  [on_device(): mine = lax.all_to_all(parts, 'col', 0, 0)]
    unnamed x41 -> x18, local copies, waits for them, and re-layouts: 15.8 us -> 2.51 us
    ppermute x36 -> x43, waiting for transfers between devices: 26.6 us -> 33.3 us  [shift(): return lax.ppermute(value, ('row', 'col'), pairs)]
    all_to_all x0 -> x1, starting transfers between devices: none -> 5.04 us  [on_device(): parts = lax.all_to_all(parts, 'col', 0, 0)]
    all_to_all x1 -> x0, other arithmetic: 2.26 us -> none  [on_device(): mine = lax.all_to_all(parts, 'col', 0, 0)]
    pallas_call x2 -> x5, Pallas kernels: 5.08 us -> 5.22 us  [the longest x1 2.41 us: prepare(): pl.pallas_call(prepare_kernel, name='prepare', compiler_params=pltpu.Comp...]
  transfers between devices with their start and end apart: 36 -> 44, of which waited for: 9 -> 7; matrix products, arithmetic and copies ran while one was open for 5% -> 1% of each run, Pallas kernels for 7% -> 10%
where the time goes in v2:
time: 171 us; the launch traced here: 169 us
  starting transfers between devices  111 us (65%)
  waiting for transfers between devices  33.3 us (19%)
  Pallas kernels  18.7 us (11%)
  local copies, waits for them, and re-layouts  3.27 us (2%)
  other arithmetic  1.9 us (1%)
    ppermute x43, starting transfers between devices, shift(): return lax.ppermute(value, ('row', 'col'), pairs)  106 us
    ppermute x43, waiting for transfers between devices, shift(): return lax.ppermute(value, ('row', 'col'), pairs)  33.3 us
    pallas_call x4, Pallas kernels, product(): pl.pallas_call(functools.partial(product_kernel, stage, sending), out_sha...  13.1 us
    all_to_all x1, starting transfers between devices, on_device(): parts = lax.all_to_all(parts, 'col', 0, 0)  5.04 us
  transfers between devices with their start and end apart: 44, of which 7 were waited for; matrix products, arithmetic and copies ran while one was open for 1% of the time, Pallas kernels for 10%

profile of v2, /device:TPU:1, one launch (start us, length us, event | category | flops | bytes accessed | tf_op | source)
XLA Modules:
  0.0 169.5 jit_solution(1068597589640650225)
XLA Ops:
  12.7 3.4 %collective-permute-start.2 = (bf16[4,96,384]{2,1,0:T(8,128)(2,1)}, bf16[4,96,384]{2,1,0:T(8,128)(2,1)S(1)}, u32[]{:S(2)}, u32[]{:S(2)}) collective-permute-start(bf16[4,96,384]{2,1,0:T(8,128)(2,1)} %get-tuple-element.21.a), channel_id=1, source_target_pairs={{0,4},{1,5},{2,6},{3,7},{4,0},{5,1},{6,2},{7,3},{8,12},{9,13},{10,... | collective-permute-start | bytes 884744 | tf_op jit(solution)/shard_map/ppermute | solution.py:23
  17.1 3.1 %collective-permute-start.20 = (bf16[384,384]{1,0:T(8,128)(2,1)S(1)}, bf16[384,384]{1,0:T(8,128)(2,1)S(1)}, u32[]{:S(2)}, u32[]{:S(2)}) collective-permute-start(bf16[384,384]{1,0:T(8,128)(2,1)S(1)} %join.1.refs_8_), channel_id=1, source_target_pairs={{0,64},{1,65},{2,66},{3,67},{4,68},{5,69},{6,70},{7,71},{8,72},{9,... | collective-permute-start | bytes 884744 | tf_op jit(solution)/shard_map/ppermute | solution.py:23
  20.8 6.0 %collective-permute-start.21 = (bf16[384,384]{1,0:T(8,128)(2,1)S(1)}, bf16[384,384]{1,0:T(8,128)(2,1)S(1)}, u32[]{:S(2)}, u32[]{:S(2)}) collective-permute-start(bf16[384,384]{1,0:T(8,128)(2,1)S(1)} %join.1.refs_8_), channel_id=1, source_target_pairs={{0,192},{1,193},{2,194},{3,195},{4,196},{5,197},{6,198},{7,199},{8... | collective-permute-start | bytes 884744 | tf_op jit(solution)/shard_map/ppermute | solution.py:23
  30.2 5.3 %collective-permute-start.23 = (bf16[384,384]{1,0:T(8,128)(2,1)S(1)}, bf16[384,384]{1,0:T(8,128)(2,1)S(1)}, u32[]{:S(2)}, u32[]{:S(2)}) collective-permute-start(bf16[384,384]{1,0:T(8,128)(2,1)S(1)} %join.1.refs_8_), channel_id=1, source_target_pairs={{0,32},{1,33},{2,34},{3,35},{4,36},{5,37},{6,38},{7,39},{8,40},{9,... | collective-permute-start | bytes 884744 | tf_op jit(solution)/shard_map/ppermute | solution.py:23
  35.5 5.6 %collective-permute-start.24 = (bf16[384,384]{1,0:T(8,128)(2,1)S(1)}, bf16[384,384]{1,0:T(8,128)(2,1)S(1)}, u32[]{:S(2)}, u32[]{:S(2)}) collective-permute-start(bf16[384,384]{1,0:T(8,128)(2,1)S(1)} %collective-permute-done.20.refs_9_), channel_id=1, source_target_pairs={{0,32},{1,33},{2,34},{3,35},{4,36},{5,37},{6,38},{7,39},{8,40},{9,... | collective-permute-start | bytes 884744 | tf_op jit(solution)/shard_map/ppermute | solution.py:23
  41.1 11.9 %collective-permute-start.25 = (bf16[384,384]{1,0:T(8,128)(2,1)S(1)}, bf16[384,384]{1,0:T(8,128)(2,1)S(1)}, u32[]{:S(2)}, u32[]{:S(2)}) collective-permute-start(bf16[384,384]{1,0:T(8,128)(2,1)S(1)} %collective-permute-done.21.refs_10_), channel_id=1, source_target_pairs={{0,32},{1,33},{2,34},{3,35},{4,36},{5,37},{6,38},{7,39},{8,40},{9,... | collective-permute-start | bytes 884744 | tf_op jit(solution)/shard_map/ppermute | solution.py:23
  53.0 2.6 %collective-permute-start.17 = (bf16[4,2,96,384]{3,2,1,0:T(8,128)(2,1)S(1)}, bf16[4,2,96,384]{3,2,1,0:T(8,128)(2,1)S(1)}, u32[]{:S(2)}, u32[]{:S(2)}) collective-permute-start(bf16[4,2,96,384]{3,2,1,0:T(8,128)(2,1)S(1)} %get-tuple-element.28.refs_4_), channel_id=1, source_target_pairs={{0,6},{1,7},{2,0},{3,1},{4,2},{5,3},{6,4},{7,5},{8,14},{9,15},{10,... | collective-permute-start | bytes 1769480 | tf_op jit(solution)/shard_map/ppermute | solution.py:23
  56.5 2.7 %collective-permute-start.14 = (bf16[4,2,96,384]{3,2,1,0:T(8,128)(2,1)S(1)}, bf16[4,2,96,384]{3,2,1,0:T(8,128)(2,1)S(1)}, u32[]{:S(2)}, u32[]{:S(2)}) collective-permute-start(bf16[4,2,96,384]{3,2,1,0:T(8,128)(2,1)S(1)} %get-tuple-element.27.refs_0_), channel_id=1, source_target_pairs={{0,24},{1,25},{2,26},{3,27},{4,28},{5,29},{6,30},{7,31},{8,0},{9,1... | collective-permute-start | bytes 1769480 | tf_op jit(solution)/shard_map/ppermute | solution.py:23
  59.2 9.5 %collective-permute-done.17.refs_6_ = bf16[4,2,96,384]{3,2,1,0:T(8,128)(2,1)S(1)} collective-permute-done((bf16[4,2,96,384]{3,2,1,0:T(8,128)(2,1)S(1)}, bf16[4,2,96,384]{3,2,1,0:T(8,128)(2,1)S(1)}, u32[]{:S(2)}, u32[]{:S(2)}) %collective-permute-start.17) | collective-permute-done | bytes 589856 | tf_op jit(solution)/shard_map/ppermute | solution.py:23
  68.6 14.8 %collective-permute-start.10 = (bf16[4,2,96,384]{3,2,1,0:T(8,128)(2,1)S(1)}, bf16[4,2,96,384]{3,2,1,0:T(8,128)(2,1)S(1)}, u32[]{:S(2)}, u32[]{:S(2)}) collective-permute-start(bf16[4,2,96,384]{3,2,1,0:T(8,128)(2,1)S(1)} %get-tuple-element.24.refs_4_), channel_id=1, source_target_pairs={{0,6},{1,7},{2,0},{3,1},{4,2},{5,3},{6,4},{7,5},{8,14},{9,15},{10,... | collective-permute-start | bytes 1769480 | tf_op jit(solution)/shard_map/ppermute | solution.py:23
  84.2 3.0 %shard_map.96 = bf16[384,384]{1,0:T(8,128)(2,1)S(1)} custom-call(bf16[4,2,96,384]{3,2,1,0:T(8,128)(2,1)S(1)} %get-tuple-element.27.refs_0_, bf16[4,2,96,384]{3,2,1,0:T(8,128)(2,1)S(1)} %collective-permute-done.13.refs_1_, bf16[4,2,96,384]{3,2,1,0:T(8,128)(2,1)S(1)} %collective-permute-done.14.refs_2_, ...), custom_call_target="tpu_custom_call" | custom-call | flops 905969664 | bytes 5000000 | tf_op jit(solution)/shard_map/pallas_call | solution.py:221
  87.2 3.2 %collective-permute-start.27 = (bf16[384,384]{1,0:T(8,128)(2,1)S(1)}, bf16[384,384]{1,0:T(8,128)(2,1)S(1)}, u32[]{:S(2)}, u32[]{:S(2)}) collective-permute-start(bf16[384,384]{1,0:T(8,128)(2,1)S(1)} %shard_map.96), channel_id=1, source_target_pairs={{0,1},{1,0},{2,3},{3,2},{4,5},{5,4},{6,7},{7,6},{8,9},{9,8},{10,11... | collective-permute-start | bytes 884744 | tf_op jit(solution)/shard_map/ppermute | solution.py:23
  93.0 6.5 %collective-permute-done.12 = bf16[192,384]{1,0:T(8,128)(2,1)S(1)} collective-permute-done((bf16[192,384]{1,0:T(8,128)(2,1)S(1)}, bf16[192,384]{1,0:T(8,128)(2,1)S(1)}, u32[]{:S(2)}, u32[]{:S(2)}) %collective-permute-start.12) | collective-permute-done | bytes 147488 | tf_op jit(solution)/shard_map/ppermute | solution.py:23
  99.8 3.0 %shard_map.95 = f32[384,384]{1,0:T(8,128)S(1)} custom-call(bf16[4,2,96,384]{3,2,1,0:T(8,128)(2,1)S(1)} %get-tuple-element.27.refs_0_, bf16[4,2,96,384]{3,2,1,0:T(8,128)(2,1)S(1)} %collective-permute-done.13.refs_1_, bf16[4,2,96,384]{3,2,1,0:T(8,128)(2,1)S(1)} %collective-permute-done.14.refs_2_, bf16[4,2,96,384]{3,2,1,0:T(8,128)(2,1)S(1)} %collective-permute-done.15.refs_3_, ...), custom_call_target="tpu_custom_call" | custom-call | flops 905969664 | bytes 5000000 | tf_op jit(solution)/shard_map/pallas_call | solution.py:221
  102.9 3.9 %collective-permute-done.10.refs_6_ = bf16[4,2,96,384]{3,2,1,0:T(8,128)(2,1)S(1)} collective-permute-done((bf16[4,2,96,384]{3,2,1,0:T(8,128)(2,1)S(1)}, bf16[4,2,96,384]{3,2,1,0:T(8,128)(2,1)S(1)}, u32[]{:S(2)}, u32[]{:S(2)}) %collective-permute-start.10) | collective-permute-done | bytes 589856 | tf_op jit(solution)/shard_map/ppermute | solution.py:23
  109.1 10.9 %collective-permute-done.9.refs_5_ = bf16[4,2,96,384]{3,2,1,0:T(8,128)(2,1)S(1)} collective-permute-done((bf16[4,2,96,384]{3,2,1,0:T(8,128)(2,1)S(1)}, bf16[4,2,96,384]{3,2,1,0:T(8,128)(2,1)S(1)}, u32[]{:S(2)}, u32[]{:S(2)}) %collective-permute-start.9) | collective-permute-done | bytes 589856 | tf_op jit(solution)/shard_map/ppermute | solution.py:23
  120.0 2.5 %collective-permute-start.36 = (bf16[192,384]{1,0:T(8,128)(2,1)}, bf16[192,384]{1,0:T(8,128)(2,1)}, u32[]{:S(2)}, u32[]{:S(2)}) collective-permute-start(bf16[192,384]{1,0:T(8,128)(2,1)} %get-tuple-element.40.refs_8_), channel_id=1, source_target_pairs={{0,192},{1,193},{2,194},{3,195},{4,196},{5,197},{6,198},{7,199},{8... | collective-permute-start | bytes 442376 | tf_op jit(solution)/shard_map/ppermute | solution.py:23
  125.6 5.0 %all-to-all-start = ((f32[32,4,128]{2,1,0:T(4,128)}), f32[32,4,128]{2,1,0:T(4,128)}, u32[]{:S(2)}, u32[]{:S(2)}) async-start(f32[32,4,128]{2,1,0:T(4,128)} %copy-done.3), calls=%async_computation | async-start | bytes 131072 | tf_op jit(solution)/shard_map/all_to_all | solution.py:341
  130.6 5.9 %collective-permute-start.38 = (bf16[192,384]{1,0:T(8,128)(2,1)}, bf16[192,384]{1,0:T(8,128)(2,1)}, u32[]{:S(2)}, u32[]{:S(2)}) collective-permute-start(bf16[192,384]{1,0:T(8,128)(2,1)} %get-tuple-element.40.refs_8_), channel_id=1, source_target_pairs={{0,32},{1,33},{2,34},{3,35},{4,36},{5,37},{6,38},{7,39},{8,40},{9,... | collective-permute-start | bytes 442376 | tf_op jit(solution)/shard_map/ppermute | solution.py:23
  140.3 2.8 %collective-permute-start.28 = (bf16[208,384]{1,0:T(8,128)(2,1)S(1)}, bf16[208,384]{1,0:T(8,128)(2,1)S(1)}, u32[]{:S(2)}, u32[]{:S(2)}) collective-permute-start(bf16[208,384]{1,0:T(8,128)(2,1)S(1)} %pad_maximum_fusion.refs_8_.refs_0_), channel_id=1, source_target_pairs={{0,64},{1,65},{2,66},{3,67},{4,68},{5,69},{6,70},{7,71},{8,72},{9,... | collective-permute-start | bytes 479240 | tf_op jit(solution)/shard_map/ppermute | solution.py:23
  143.9 4.3 %collective-permute-start.30 = (bf16[208,384]{1,0:T(8,128)(2,1)S(1)}, bf16[208,384]{1,0:T(8,128)(2,1)S(1)}, u32[]{:S(2)}, u32[]{:S(2)}) collective-permute-start(bf16[208,384]{1,0:T(8,128)(2,1)S(1)} %pad_maximum_fusion.refs_8_.refs_0_), channel_id=1, source_target_pairs={{0,128},{1,129},{2,130},{3,131},{4,132},{5,133},{6,134},{7,135},{8... | collective-permute-start | bytes 479240 | tf_op jit(solution)/shard_map/ppermute | solution.py:23
  148.3 3.9 %shard_map.98 = bf16[192,768]{1,0:T(8,128)(2,1)S(1)} custom-call(bf16[4,2,96,384]{3,2,1,0:T(8,128)(2,1)S(1)} %get-tuple-element.22.refs_0_, bf16[4,2,96,384]{3,2,1,0:T(8,128)(2,1)S(1)} %collective-permute-done.3.refs_1_, bf16[4,2,96,384]{3,2,1,0:T(8,128)(2,1)} %collective-permute-done.4.refs_2_, bf16[4,2,96,384]{3,2,1,0:T(8,128)(2,1)} %collective-permute-done.5.refs_3_, ...), custom_call_target="tpu_custom_call" | custom-call | flops 905969664 | bytes 5000000 | tf_op jit(solution)/shard_map/pallas_call | solution.py:221
  153.7 7.5 %collective-permute-start.31 = (bf16[208,384]{1,0:T(8,128)(2,1)S(1)}, bf16[208,384]{1,0:T(8,128)(2,1)S(1)}, u32[]{:S(2)}, u32[]{:S(2)}) collective-permute-start(bf16[208,384]{1,0:T(8,128)(2,1)S(1)} %pad_maximum_fusion.refs_8_.refs_0_), channel_id=1, source_target_pairs={{0,32},{1,33},{2,34},{3,35},{4,36},{5,37},{6,38},{7,39},{8,40},{9,... | collective-permute-start | bytes 479240 | tf_op jit(solution)/shard_map/ppermute | solution.py:23
  164.6 3.2 %shard_map.97 = f32[192,768]{1,0:T(8,128)S(1)} custom-call(bf16[4,2,96,384]{3,2,1,0:T(8,128)(2,1)S(1)} %get-tuple-element.22.refs_0_, bf16[4,2,96,384]{3,2,1,0:T(8,128)(2,1)S(1)} %collective-permute-done.3.refs_1_, bf16[4,2,96,384]{3,2,1,0:T(8,128)(2,1)} %collective-permute-done.4.refs_2_, bf16[4,2,96,384]{3,2,1,0:T(8,128)(2,1)} %collective-permute-done.5.refs_3_, ...), custom_call_target="tpu_custom_call" | custom-call | flops 905969664 | bytes 5000000 | tf_op jit(solution)/shard_map/pallas_call | solution.py:221
  (97 shorter events, 38.2 us)
Async XLA Ops:
  9.9 18.1 %collective-permute-start = (bf16[4,96,384]{2,1,0:T(8,128)(2,1)}, bf16[4,96,384]{2,1,0:T(8,128)(2,1)S(1)}, u32[]{:S(2)}, u32[]{:S(2)}) collective-permute-start(bf16[4,96,384]{2,1,0:T(8,128)(2,1)} %get-tuple-element.21.a), channel_id=1, source_target_pairs={{0,2},{1,3},{2,4},{3,5},{4,6},{5,7},{6,0},{7,1},{8,10},{9,11},{10,... | collective-permute-start | bytes 884744 | tf_op jit(solution)/shard_map/ppermute | solution.py:23
  11.1 17.9 %collective-permute-start.1 = (bf16[4,96,384]{2,1,0:T(8,128)(2,1)}, bf16[4,96,384]{2,1,0:T(8,128)(2,1)S(1)}, u32[]{:S(2)}, u32[]{:S(2)}) collective-permute-start(bf16[4,96,384]{2,1,0:T(8,128)(2,1)} %get-tuple-element.21.a), channel_id=1, source_target_pairs={{0,6},{1,7},{2,0},{3,1},{4,2},{5,3},{6,4},{7,5},{8,14},{9,15},{10,... | collective-permute-start | bytes 884744 | tf_op jit(solution)/shard_map/ppermute | solution.py:23
  12.7 17.5 %collective-permute-start.2 = (bf16[4,96,384]{2,1,0:T(8,128)(2,1)}, bf16[4,96,384]{2,1,0:T(8,128)(2,1)S(1)}, u32[]{:S(2)}, u32[]{:S(2)}) collective-permute-start(bf16[4,96,384]{2,1,0:T(8,128)(2,1)} %get-tuple-element.21.a), channel_id=1, source_target_pairs={{0,4},{1,5},{2,6},{3,7},{4,0},{5,1},{6,2},{7,3},{8,12},{9,13},{10,... | collective-permute-start | bytes 884744 | tf_op jit(solution)/shard_map/ppermute | solution.py:23
  17.1 18.4 %collective-permute-start.20 = (bf16[384,384]{1,0:T(8,128)(2,1)S(1)}, bf16[384,384]{1,0:T(8,128)(2,1)S(1)}, u32[]{:S(2)}, u32[]{:S(2)}) collective-permute-start(bf16[384,384]{1,0:T(8,128)(2,1)S(1)} %join.1.refs_8_), channel_id=1, source_target_pairs={{0,64},{1,65},{2,66},{3,67},{4,68},{5,69},{6,70},{7,71},{8,72},{9,... | collective-permute-start | bytes 884744 | tf_op jit(solution)/shard_map/ppermute | solution.py:23
  20.8 20.4 %collective-permute-start.21 = (bf16[384,384]{1,0:T(8,128)(2,1)S(1)}, bf16[384,384]{1,0:T(8,128)(2,1)S(1)}, u32[]{:S(2)}, u32[]{:S(2)}) collective-permute-start(bf16[384,384]{1,0:T(8,128)(2,1)S(1)} %join.1.refs_8_), channel_id=1, source_target_pairs={{0,192},{1,193},{2,194},{3,195},{4,196},{5,197},{6,198},{7,199},{8... | collective-permute-start | bytes 884744 | tf_op jit(solution)/shard_map/ppermute | solution.py:23
  28.0 25.0 %collective-permute-start.22 = (bf16[384,384]{1,0:T(8,128)(2,1)S(1)}, bf16[384,384]{1,0:T(8,128)(2,1)S(1)}, u32[]{:S(2)}, u32[]{:S(2)}) collective-permute-start(bf16[384,384]{1,0:T(8,128)(2,1)S(1)} %join.1.refs_8_), channel_id=1, source_target_pairs={{0,128},{1,129},{2,130},{3,131},{4,132},{5,133},{6,134},{7,135},{8... | collective-permute-start | bytes 884744 | tf_op jit(solution)/shard_map/ppermute | solution.py:23
  29.0 30.1 %collective-permute-start.16 = (bf16[4,2,96,384]{3,2,1,0:T(8,128)(2,1)S(1)}, bf16[4,2,96,384]{3,2,1,0:T(8,128)(2,1)S(1)}, u32[]{:S(2)}, u32[]{:S(2)}) collective-permute-start(bf16[4,2,96,384]{3,2,1,0:T(8,128)(2,1)S(1)} %get-tuple-element.28.refs_4_), channel_id=1, source_target_pairs={{0,2},{1,3},{2,4},{3,5},{4,6},{5,7},{6,0},{7,1},{8,10},{9,11},{10,... | collective-permute-start | bytes 1769480 | tf_op jit(solution)/shard_map/ppermute | solution.py:23
  30.2 22.8 %collective-permute-start.23 = (bf16[384,384]{1,0:T(8,128)(2,1)S(1)}, bf16[384,384]{1,0:T(8,128)(2,1)S(1)}, u32[]{:S(2)}, u32[]{:S(2)}) collective-permute-start(bf16[384,384]{1,0:T(8,128)(2,1)S(1)} %join.1.refs_8_), channel_id=1, source_target_pairs={{0,32},{1,33},{2,34},{3,35},{4,36},{5,37},{6,38},{7,39},{8,40},{9,... | collective-permute-start | bytes 884744 | tf_op jit(solution)/shard_map/ppermute | solution.py:23
  35.5 20.3 %collective-permute-start.24 = (bf16[384,384]{1,0:T(8,128)(2,1)S(1)}, bf16[384,384]{1,0:T(8,128)(2,1)S(1)}, u32[]{:S(2)}, u32[]{:S(2)}) collective-permute-start(bf16[384,384]{1,0:T(8,128)(2,1)S(1)} %collective-permute-done.20.refs_9_), channel_id=1, source_target_pairs={{0,32},{1,33},{2,34},{3,35},{4,36},{5,37},{6,38},{7,39},{8,40},{9,... | collective-permute-start | bytes 884744 | tf_op jit(solution)/shard_map/ppermute | solution.py:23
  55.9 27.5 %collective-permute-start.18 = (bf16[4,2,96,384]{3,2,1,0:T(8,128)(2,1)S(1)}, bf16[4,2,96,384]{3,2,1,0:T(8,128)(2,1)S(1)}, u32[]{:S(2)}, u32[]{:S(2)}) collective-permute-start(bf16[4,2,96,384]{3,2,1,0:T(8,128)(2,1)S(1)} %get-tuple-element.28.refs_4_), channel_id=1, source_target_pairs={{0,4},{1,5},{2,6},{3,7},{4,0},{5,1},{6,2},{7,3},{8,12},{9,13},{10,... | collective-permute-start | bytes 1769480 | tf_op jit(solution)/shard_map/ppermute | solution.py:23
  56.5 27.7 %collective-permute-start.13 = (bf16[4,2,96,384]{3,2,1,0:T(8,128)(2,1)S(1)}, bf16[4,2,96,384]{3,2,1,0:T(8,128)(2,1)S(1)}, u32[]{:S(2)}, u32[]{:S(2)}) collective-permute-start(bf16[4,2,96,384]{3,2,1,0:T(8,128)(2,1)S(1)} %get-tuple-element.27.refs_0_), channel_id=1, source_target_pairs={{0,8},{1,9},{2,10},{3,11},{4,12},{5,13},{6,14},{7,15},{8,16},{9,17... | collective-permute-start | bytes 1769480 | tf_op jit(solution)/shard_map/ppermute | solution.py:23
  56.5 27.7 %collective-permute-start.14 = (bf16[4,2,96,384]{3,2,1,0:T(8,128)(2,1)S(1)}, bf16[4,2,96,384]{3,2,1,0:T(8,128)(2,1)S(1)}, u32[]{:S(2)}, u32[]{:S(2)}) collective-permute-start(bf16[4,2,96,384]{3,2,1,0:T(8,128)(2,1)S(1)} %get-tuple-element.27.refs_0_), channel_id=1, source_target_pairs={{0,24},{1,25},{2,26},{3,27},{4,28},{5,29},{6,30},{7,31},{8,0},{9,1... | collective-permute-start | bytes 1769480 | tf_op jit(solution)/shard_map/ppermute | solution.py:23
  59.1 25.1 %collective-permute-start.15 = (bf16[4,2,96,384]{3,2,1,0:T(8,128)(2,1)S(1)}, bf16[4,2,96,384]{3,2,1,0:T(8,128)(2,1)S(1)}, u32[]{:S(2)}, u32[]{:S(2)}) collective-permute-start(bf16[4,2,96,384]{3,2,1,0:T(8,128)(2,1)S(1)} %get-tuple-element.27.refs_0_), channel_id=1, source_target_pairs={{0,16},{1,17},{2,18},{3,19},{4,20},{5,21},{6,22},{7,23},{8,24},{9,... | collective-permute-start | bytes 1769480 | tf_op jit(solution)/shard_map/ppermute | solution.py:23
  68.6 38.1 %collective-permute-start.10 = (bf16[4,2,96,384]{3,2,1,0:T(8,128)(2,1)S(1)}, bf16[4,2,96,384]{3,2,1,0:T(8,128)(2,1)S(1)}, u32[]{:S(2)}, u32[]{:S(2)}) collective-permute-start(bf16[4,2,96,384]{3,2,1,0:T(8,128)(2,1)S(1)} %get-tuple-element.24.refs_4_), channel_id=1, source_target_pairs={{0,6},{1,7},{2,0},{3,1},{4,2},{5,3},{6,4},{7,5},{8,14},{9,15},{10,... | collective-permute-start | bytes 1769480 | tf_op jit(solution)/shard_map/ppermute | solution.py:23
  87.2 19.9 %collective-permute-start.27 = (bf16[384,384]{1,0:T(8,128)(2,1)S(1)}, bf16[384,384]{1,0:T(8,128)(2,1)S(1)}, u32[]{:S(2)}, u32[]{:S(2)}) collective-permute-start(bf16[384,384]{1,0:T(8,128)(2,1)S(1)} %shard_map.96), channel_id=1, source_target_pairs={{0,1},{1,0},{2,3},{3,2},{4,5},{5,4},{6,7},{7,6},{8,9},{9,8},{10,11... | collective-permute-start | bytes 884744 | tf_op jit(solution)/shard_map/ppermute | solution.py:23
  90.5 18.5 %collective-permute-start.11 = (bf16[4,2,96,384]{3,2,1,0:T(8,128)(2,1)S(1)}, bf16[4,2,96,384]{3,2,1,0:T(8,128)(2,1)S(1)}, u32[]{:S(2)}, u32[]{:S(2)}) collective-permute-start(bf16[4,2,96,384]{3,2,1,0:T(8,128)(2,1)S(1)} %get-tuple-element.24.refs_4_), channel_id=1, source_target_pairs={{0,4},{1,5},{2,6},{3,7},{4,0},{5,1},{6,2},{7,3},{8,12},{9,13},{10,... | collective-permute-start | bytes 1769480 | tf_op jit(solution)/shard_map/ppermute | solution.py:23
  93.0 27.0 %collective-permute-start.9 = (bf16[4,2,96,384]{3,2,1,0:T(8,128)(2,1)S(1)}, bf16[4,2,96,384]{3,2,1,0:T(8,128)(2,1)S(1)}, u32[]{:S(2)}, u32[]{:S(2)}) collective-permute-start(bf16[4,2,96,384]{3,2,1,0:T(8,128)(2,1)S(1)} %get-tuple-element.24.refs_4_), channel_id=1, source_target_pairs={{0,2},{1,3},{2,4},{3,5},{4,6},{5,7},{6,0},{7,1},{8,10},{9,11},{10,... | collective-permute-start | bytes 1769480 | tf_op jit(solution)/shard_map/ppermute | solution.py:23
  99.5 23.1 %collective-permute-start.3 = (bf16[4,2,96,384]{3,2,1,0:T(8,128)(2,1)S(1)}, bf16[4,2,96,384]{3,2,1,0:T(8,128)(2,1)S(1)}, u32[]{:S(2)}, u32[]{:S(2)}) collective-permute-start(bf16[4,2,96,384]{3,2,1,0:T(8,128)(2,1)S(1)} %get-tuple-element.22.refs_0_), channel_id=1, source_target_pairs={{0,8},{1,9},{2,10},{3,11},{4,12},{5,13},{6,14},{7,15},{8,16},{9,17... | collective-permute-start | bytes 1769480 | tf_op jit(solution)/shard_map/ppermute | solution.py:23
  106.8 23.9 %collective-permute-start.4 = (bf16[4,2,96,384]{3,2,1,0:T(8,128)(2,1)S(1)}, bf16[4,2,96,384]{3,2,1,0:T(8,128)(2,1)}, u32[]{:S(2)}, u32[]{:S(2)}) collective-permute-start(bf16[4,2,96,384]{3,2,1,0:T(8,128)(2,1)S(1)} %get-tuple-element.22.refs_0_), channel_id=1, source_target_pairs={{0,24},{1,25},{2,26},{3,27},{4,28},{5,29},{6,30},{7,31},{8,0},{9,1... | collective-permute-start | bytes 1769480 | tf_op jit(solution)/shard_map/ppermute | solution.py:23
  107.1 33.2 %collective-permute-start.5 = (bf16[4,2,96,384]{3,2,1,0:T(8,128)(2,1)S(1)}, bf16[4,2,96,384]{3,2,1,0:T(8,128)(2,1)}, u32[]{:S(2)}, u32[]{:S(2)}) collective-permute-start(bf16[4,2,96,384]{3,2,1,0:T(8,128)(2,1)S(1)} %get-tuple-element.22.refs_0_), channel_id=1, source_target_pairs={{0,16},{1,17},{2,18},{3,19},{4,20},{5,21},{6,22},{7,23},{8,24},{9,... | collective-permute-start | bytes 1769480 | tf_op jit(solution)/shard_map/ppermute | solution.py:23
  109.1 27.5 %collective-permute-start.35 = (bf16[192,384]{1,0:T(8,128)(2,1)}, bf16[192,384]{1,0:T(8,128)(2,1)}, u32[]{:S(2)}, u32[]{:S(2)}) collective-permute-start(bf16[192,384]{1,0:T(8,128)(2,1)} %get-tuple-element.40.refs_8_), channel_id=1, source_target_pairs={{0,64},{1,65},{2,66},{3,67},{4,68},{5,69},{6,70},{7,71},{8,72},{9,... | collective-permute-start | bytes 442376 | tf_op jit(solution)/shard_map/ppermute | solution.py:23
  140.3 21.0 %collective-permute-start.28 = (bf16[208,384]{1,0:T(8,128)(2,1)S(1)}, bf16[208,384]{1,0:T(8,128)(2,1)S(1)}, u32[]{:S(2)}, u32[]{:S(2)}) collective-permute-start(bf16[208,384]{1,0:T(8,128)(2,1)S(1)} %pad_maximum_fusion.refs_8_.refs_0_), channel_id=1, source_target_pairs={{0,64},{1,65},{2,66},{3,67},{4,68},{5,69},{6,70},{7,71},{8,72},{9,... | collective-permute-start | bytes 479240 | tf_op jit(solution)/shard_map/ppermute | solution.py:23
  143.0 18.2 %collective-permute-start.29 = (bf16[208,384]{1,0:T(8,128)(2,1)S(1)}, bf16[208,384]{1,0:T(8,128)(2,1)S(1)}, u32[]{:S(2)}, u32[]{:S(2)}) collective-permute-start(bf16[208,384]{1,0:T(8,128)(2,1)S(1)} %pad_maximum_fusion.refs_8_.refs_0_), channel_id=1, source_target_pairs={{0,192},{1,193},{2,194},{3,195},{4,196},{5,197},{6,198},{7,199},{8... | collective-permute-start | bytes 479240 | tf_op jit(solution)/shard_map/ppermute | solution.py:23
  143.9 17.8 %collective-permute-start.30 = (bf16[208,384]{1,0:T(8,128)(2,1)S(1)}, bf16[208,384]{1,0:T(8,128)(2,1)S(1)}, u32[]{:S(2)}, u32[]{:S(2)}) collective-permute-start(bf16[208,384]{1,0:T(8,128)(2,1)S(1)} %pad_maximum_fusion.refs_8_.refs_0_), channel_id=1, source_target_pairs={{0,128},{1,129},{2,130},{3,131},{4,132},{5,133},{6,134},{7,135},{8... | collective-permute-start | bytes 479240 | tf_op jit(solution)/shard_map/ppermute | solution.py:23
  (29 other events, 350.7 us)

commit v3 on v2

--- a/solution.py
+++ b/solution.py
@@ -45,7 +45,7 @@
     ]
 
 
-def prepare_kernel(v_ref, a_ref, b_ref, im_ref, am_ref, va1, va2, b_out, keep, send_a, send_b):
+def prepare_kernel(v_ref, a_ref, b_ref, im_ref, am_ref, va1, va2, b_out, keep, send):
     low = lax.broadcasted_iota(jnp.int32, (TILE, 128), 1) < TILE
     zl = lax.axis_index("col") % 2
     for which, (ref, mask) in enumerate(((v_ref, im_ref), (a_ref, am_ref), (b_ref, im_ref))):
@@ -80,7 +80,7 @@
                 for t in range(3):
                     lanes = slice(t * 128, t * 128 + 128)
                     into[rows, lanes] = jnp.where(zl == 0, tiles[t], tiles[t + 3])
-                    (send_a if which == 1 else send_b)[rows, lanes] = jnp.where(zl == 0, tiles[t + 3], tiles[t])
+                    send[which - 1, rows, lanes] = jnp.where(zl == 0, tiles[t + 3], tiles[t])
 
 
 VMEM = pl.BlockSpec(memory_space=pltpu.VMEM)
@@ -99,18 +99,17 @@
             struct((4, 96, 384), BF16),
             struct((192, 384), BF16),
             struct((192, 384), BF16),
-            struct((192, 384), BF16),
-            struct((192, 384), BF16),
+            struct((2, 192, 384), BF16),
         ),
         in_specs=[VMEM, VMEM, VMEM, SMEM, SMEM],
-        out_specs=(VMEM,) * 6,
+        out_specs=(VMEM,) * 5,
         cost_estimate=pl.CostEstimate(flops=10**6, bytes_accessed=2 * 10**6, transcendentals=0),
     )(vt, at, bt, int_mask, amp_mask)
 
 
 def join_kernel(a, b, out, sem):
     copies = []
-    for i, ref in enumerate((a, b)):
+    for i, ref in enumerate((a, b.at[0])):
         for lane in (0, 128, 256):
             lanes = pl.ds(lane, 128)
             into = out.at[pl.ds(192 * i, 192), lanes]
@@ -165,7 +164,7 @@
 
 
 def product_kernel(stage, sending, *refs):
-    stacks, pieces, (out, w, g, total, w_sems, g_sems) = refs[:8], refs[8:16], refs[16:]
+    stacks, pieces, (*outs, w, g, total, w_sems, g_sems) = refs[:8], refs[8:16], refs[16:]
     zh, core, y, x, _ = place()
     count = g.shape[1]
     sides = ((0 if sending else 1),) if stage == 1 else (0, 1)
@@ -204,25 +203,25 @@
         total[...] += jnp.dot(g[k], w[part, :], preferred_element_type=F32)
 
     if stage == 2:
+        (out,) = outs
         for k in range(3):
             part = slice(k * 64, k * 64 + 64)
             tiles = swap_middle([total[part, t * 128 : t * 128 + 128] for t in range(6)])
             for t, v in enumerate(tiles):
                 out[part, t * 128 : t * 128 + 128] = v.astype(out.dtype)
-    elif sending:
-        out[0:192, :] = total[192:384].astype(BF16)
-        out[192:384, :] = total[0:192].astype(BF16)
     else:
-        out[...] = total[...]
+        own, away = total[0:192], total[192:384]
+        outs[0][...] = (own if sending else away).astype(outs[0].dtype)
+        outs[1][...] = (away if sending else own).astype(outs[1].dtype)
 
 
 def product(stage, sending, stacks, pieces):
     rows, width = (384, 384) if stage == 1 else (192, 768)
     return pl.pallas_call(
         functools.partial(product_kernel, stage, sending),
-        out_shape=jax.ShapeDtypeStruct((rows, width), BF16 if sending else F32),
+        out_shape=(jax.ShapeDtypeStruct((192, width), BF16 if sending else F32),) * (3 - stage),
         in_specs=[ANY] * 16,
-        out_specs=VMEM,
+        out_specs=(VMEM,) * (3 - stage),
         scratch_shapes=[
             pltpu.VMEM((3072, width), BF16),
             pltpu.VMEM((4, rows, 768), BF16),
@@ -237,8 +236,11 @@
     )(*stacks, *pieces)
 
 
-def right_operand(piece):
-    mine = ring(piece, "zh")
+def right_operand(piece, via):
+    before = shift(piece, zh=1)
+    after = shift(piece, zh=-1)
+    far = shift(after, zh=-1) if via < 0 else shift(before, zh=1)
+    mine = [piece, before, after, far]
     return mine + [shift(v, core=1) for v in mine]
 
 
@@ -323,31 +325,32 @@
 def on_device(
     tile_amps, cycle_ints, base_ints, amp_mask, int_mask, pair_amps, ladder_ints, pair_list
 ):
-    va1, va2, base, keep, send_a, send_b = prepare(
+    va1, va2, base, keep, send = prepare(
         cycle_ints.T, tile_amps.T, base_ints.T, int_mask.T, amp_mask.T
     )
-    came = shift(send_a, zl=1)
+    swapped = shift(send, zl=1)
     x_blocks, y_blocks = ring(va1, "x"), ring(va2, "y")
-    right = right_operand(join(keep, came))
+    right = right_operand(join(keep, swapped), -1)
     ints1, amps1 = stack(x_blocks)
     ints2, amps2 = stack(y_blocks)
     stacks = ring(ints1, "y") + ring(ints2, "x")
     send = product(1, True, stacks, right)
-    came = shift(send, zl=1)
+    came = [shift(v, zl=1) for v in send]
     keep = product(1, False, stacks, right)
-    base = jnp.concatenate([base, shift(send_b, zl=1)], axis=0)
-
+    bases = [swapped[1], base]
     parts = ladder_part(pair_amps, ladder_ints, pair_list)
     parts = lax.all_to_all(parts, "col", 0, 0)
     rows = ladder_sum(parts)
 
     stacks = ring(amps1, "y") + ring(amps2, "x")
-    piece = (base.astype(F32) + (keep + came.astype(F32))).astype(BF16)
-    away = right_operand(piece[192:])
-    mine = right_operand(jnp.concatenate([piece[:192], rows], axis=0))
-    send = product(2, True, stacks, away)
+    pieces = [
+        (b.astype(F32) + (k + c.astype(F32))).astype(BF16) for b, k, c in zip(bases, keep, came)
+    ]
+    away = right_operand(pieces[0], -1)
+    mine = right_operand(jnp.concatenate([pieces[1], rows], axis=0), 1)
+    (send,) = product(2, True, stacks, away)
     came = shift(send, zl=1)
-    keep = product(2, False, stacks, mine)
+    (keep,) = product(2, False, stacks, mine)
     keep, *mine = lax.optimization_barrier((keep, *mine))
     ladder = ladder_end(mine)
     return (keep + came.astype(F32)).T, ladder

time: 171 us -> 173 us (1.012)
  local copies, waits for them, and re-layouts: 3.27 us -> 29.1 us
  starting transfers between devices: 111 us -> 86.7 us
    ppermute x43, starting transfers between devices: 106 us -> 78.8 us  [shift(): return lax.ppermute(value, ('row', 'col'), pairs)]
    unnamed x18 -> x76, local copies, waits for them, and re-layouts: 2.51 us -> 29.1 us
    all_to_all x1, starting transfers between devices: 5.04 us -> 7.89 us  [on_device(): parts = lax.all_to_all(parts, 'col', 0, 0)]
  transfers between devices with their start and end apart: 44 -> 44, of which waited for: 7 -> 10; matrix products, arithmetic and copies ran while one was open for 1% -> 1% of each run, Pallas kernels for 10% -> 10%
where the time goes in v3:
time: 173 us; the launch traced here: 172 us
  starting transfers between devices  86.7 us (50%)
  waiting for transfers between devices  33.9 us (20%)
  local copies, waits for them, and re-layouts  29.1 us (17%)
  Pallas kernels  19.6 us (11%)
  other arithmetic  1.9 us (1%)
    ppermute x43, starting transfers between devices, shift(): return lax.ppermute(value, ('row', 'col'), pairs)  78.8 us
    ppermute x43, waiting for transfers between devices, shift(): return lax.ppermute(value, ('row', 'col'), pairs)  33.9 us
    unnamed x76, local copies, waits for them, and re-layouts  29.1 us
    pallas_call x4, Pallas kernels, product(): pl.pallas_call(functools.partial(product_kernel, stage, sending), out_sha...  13.8 us
    all_to_all x1, starting transfers between devices, on_device(): parts = lax.all_to_all(parts, 'col', 0, 0)  7.89 us
  transfers between devices with their start and end apart: 44, of which 10 were waited for; matrix products, arithmetic and copies ran while one was open for 1% of the time, Pallas kernels for 10%

profile of v3, /device:TPU:1, one launch (start us, length us, event | category | flops | bytes accessed | tf_op | source)
XLA Modules:
  0.0 172.2 jit_solution(13487992696380796294)
XLA Ops:
  0.6 2.4 %prepare.1 = (bf16[4,96,384]{2,1,0:T(8,128)(2,1)}, bf16[4,96,384]{2,1,0:T(8,128)(2,1)}, bf16[192,384]{1,0:T(8,128)(2,1)}, bf16[192,384]{1,0:T(8,128)(2,1)}, bf16[2,192,384]{2,1,0:T(8,128)(2,1)}) custom-call(bf16[192,768]{1,0:T(8,128)(2,1)} %bitcast.12, bf16[192,768]{1,0:T(8,128)(2,1)} %bitcast.13, bf16[192,768]{1,0:T(8,128)(2,1)} %bitcast.14, ...), custom_call_target="tpu_custom_call" | custom-call | flops 1000000 | bytes 2000000 | tf_op jit(solution)/shard_map/prepare/pallas_call | solution.py:93
  11.7 4.2 %collective-permute-start.1 = (bf16[4,96,384]{2,1,0:T(8,128)(2,1)}, bf16[4,96,384]{2,1,0:T(8,128)(2,1)S(1)}, u32[]{:S(2)}, u32[]{:S(2)}) collective-permute-start(bf16[4,96,384]{2,1,0:T(8,128)(2,1)} %get-tuple-element.24.a), channel_id=1, source_target_pairs={{0,6},{1,7},{2,0},{3,1},{4,2},{5,3},{6,4},{7,5},{8,14},{9,15},{10,... | collective-permute-start | bytes 884744 | tf_op jit(solution)/shard_map/ppermute | solution.py:23
  15.9 5.0 %collective-permute-done.8.d = bf16[4,96,384]{2,1,0:T(8,128)(2,1)S(1)} collective-permute-done((bf16[4,96,384]{2,1,0:T(8,128)(2,1)}, bf16[4,96,384]{2,1,0:T(8,128)(2,1)S(1)}, u32[]{:S(2)}, u32[]{:S(2)}) %collective-permute-start.8) | collective-permute-done | bytes 294944 | tf_op jit(solution)/shard_map/ppermute | solution.py:23
  23.3 2.5 %collective-permute-start.2 = (bf16[4,96,384]{2,1,0:T(8,128)(2,1)}, bf16[4,96,384]{2,1,0:T(8,128)(2,1)S(1)}, u32[]{:S(2)}, u32[]{:S(2)}) collective-permute-start(bf16[4,96,384]{2,1,0:T(8,128)(2,1)} %get-tuple-element.24.a), channel_id=1, source_target_pairs={{0,4},{1,5},{2,6},{3,7},{4,0},{5,1},{6,2},{7,3},{8,12},{9,13},{10,... | collective-permute-start | bytes 884744 | tf_op jit(solution)/shard_map/ppermute | solution.py:23
  27.5 6.0 %collective-permute-start.20 = (bf16[384,384]{1,0:T(8,128)(2,1)S(1)}, bf16[384,384]{1,0:T(8,128)(2,1)S(1)}, u32[]{:S(2)}, u32[]{:S(2)}) collective-permute-start(bf16[384,384]{1,0:T(8,128)(2,1)S(1)} %join.1.refs_8_), channel_id=1, source_target_pairs={{0,192},{1,193},{2,194},{3,195},{4,196},{5,197},{6,198},{7,199},{8... | collective-permute-start | bytes 884744 | tf_op jit(solution)/shard_map/ppermute | solution.py:23
  33.5 2.5 %collective-permute-start.22 = (bf16[384,384]{1,0:T(8,128)(2,1)S(1)}, bf16[384,384]{1,0:T(8,128)(2,1)S(1)}, u32[]{:S(2)}, u32[]{:S(2)}) collective-permute-start(bf16[384,384]{1,0:T(8,128)(2,1)S(1)} %join.1.refs_8_), channel_id=1, source_target_pairs={{0,32},{1,33},{2,34},{3,35},{4,36},{5,37},{6,38},{7,39},{8,40},{9,... | collective-permute-start | bytes 884744 | tf_op jit(solution)/shard_map/ppermute | solution.py:23
  36.0 8.1 %collective-permute-done.2.d = bf16[4,96,384]{2,1,0:T(8,128)(2,1)S(1)} collective-permute-done((bf16[4,96,384]{2,1,0:T(8,128)(2,1)}, bf16[4,96,384]{2,1,0:T(8,128)(2,1)S(1)}, u32[]{:S(2)}, u32[]{:S(2)}) %collective-permute-start.2) | collective-permute-done | bytes 294944 | tf_op jit(solution)/shard_map/ppermute | solution.py:23
  46.0 2.4 %collective-permute-start.13 = (bf16[4,2,96,384]{3,2,1,0:T(8,128)(2,1)S(1)}, bf16[4,2,96,384]{3,2,1,0:T(8,128)(2,1)S(1)}, u32[]{:S(2)}, u32[]{:S(2)}) collective-permute-start(bf16[4,2,96,384]{3,2,1,0:T(8,128)(2,1)S(1)} %get-tuple-element.29.refs_0_), channel_id=1, source_target_pairs={{0,24},{1,25},{2,26},{3,27},{4,28},{5,29},{6,30},{7,31},{8,0},{9,1... | collective-permute-start | bytes 1769480 | tf_op jit(solution)/shard_map/ppermute | solution.py:23
  50.0 6.7 %collective-permute-done.16.refs_6_ = bf16[4,2,96,384]{3,2,1,0:T(8,128)(2,1)S(1)} collective-permute-done((bf16[4,2,96,384]{3,2,1,0:T(8,128)(2,1)S(1)}, bf16[4,2,96,384]{3,2,1,0:T(8,128)(2,1)S(1)}, u32[]{:S(2)}, u32[]{:S(2)}) %collective-permute-start.16) | collective-permute-done | bytes 589856 | tf_op jit(solution)/shard_map/ppermute | solution.py:23
  57.5 5.8 %collective-permute-start.21 = (bf16[384,384]{1,0:T(8,128)(2,1)S(1)}, bf16[384,384]{1,0:T(8,128)(2,1)}, u32[]{:S(2)}, u32[]{:S(2)}) collective-permute-start(bf16[384,384]{1,0:T(8,128)(2,1)S(1)} %collective-permute-done.20.refs_10_), channel_id=1, source_target_pairs={{0,192},{1,193},{2,194},{3,195},{4,196},{5,197},{6,198},{7,199},{8... | collective-permute-start | bytes 884744 | tf_op jit(solution)/shard_map/ppermute | solution.py:23
  64.2 8.4 %collective-permute-start.10 = (bf16[4,2,96,384]{3,2,1,0:T(8,128)(2,1)S(1)}, bf16[4,2,96,384]{3,2,1,0:T(8,128)(2,1)S(1)}, u32[]{:S(2)}, u32[]{:S(2)}) collective-permute-start(bf16[4,2,96,384]{3,2,1,0:T(8,128)(2,1)S(1)} %get-tuple-element.27.refs_4_), channel_id=1, source_target_pairs={{0,6},{1,7},{2,0},{3,1},{4,2},{5,3},{6,4},{7,5},{8,14},{9,15},{10,... | collective-permute-start | bytes 1769480 | tf_op jit(solution)/shard_map/ppermute | solution.py:23
  74.2 4.7 %collective-permute-start.24 = (bf16[384,384]{1,0:T(8,128)(2,1)S(1)}, bf16[384,384]{1,0:T(8,128)(2,1)}, u32[]{:S(2)}, u32[]{:S(2)}) collective-permute-start(bf16[384,384]{1,0:T(8,128)(2,1)S(1)} %collective-permute-done.20.refs_10_), channel_id=1, source_target_pairs={{0,32},{1,33},{2,34},{3,35},{4,36},{5,37},{6,38},{7,39},{8,40},{9,... | collective-permute-start | bytes 884744 | tf_op jit(solution)/shard_map/ppermute | solution.py:23
  82.8 7.9 %all-to-all-start = ((f32[32,4,128]{2,1,0:T(4,128)}), f32[32,4,128]{2,1,0:T(4,128)}, u32[]{:S(2)}, u32[]{:S(2)}) async-start(f32[32,4,128]{2,1,0:T(4,128)} %copy-done.31), calls=%async_computation | async-start | bytes 131072 | tf_op jit(solution)/shard_map/all_to_all | solution.py:342
  99.2 4.1 %shard_map.96 = (bf16[192,384]{1,0:T(8,128)(2,1)}, bf16[192,384]{1,0:T(8,128)(2,1)S(1)}) custom-call(bf16[4,2,96,384]{3,2,1,0:T(8,128)(2,1)S(1)} %copy-done.9, bf16[4,2,96,384]{3,2,1,0:T(8,128)(2,1)S(1)} %copy-done.15, bf16[4,2,96,384]{3,2,1,0:T(8,128)(2,1)S(1)} %copy-done.18, bf16[4,2,96,384]{3,2,1,0:T(8,128)(2,1)S(1)} %copy-done.21, ...), custom_call_target="tpu_custom_call" | custom-call | flops 905969664 | bytes 5000000 | tf_op jit(solution)/shard_map/pallas_call | solution.py:220
  117.9 3.4 %shard_map.95 = (f32[192,384]{1,0:T(8,128)S(1)}, f32[192,384]{1,0:T(8,128)S(1)}) custom-call(bf16[4,2,96,384]{3,2,1,0:T(8,128)(2,1)S(1)} %copy-done.10, bf16[4,2,96,384]{3,2,1,0:T(8,128)(2,1)S(1)} %copy-done.16, bf16[4,2,96,384]{3,2,1,0:T(8,128)(2,1)S(1)} %copy-done.19, bf16[4,2,96,384]{3,2,1,0:T(8,128)(2,1)S(1)} %copy-done.22, ...), custom_call_target="tpu_custom_call" | custom-call | flops 905969664 | bytes 5000000 | tf_op jit(solution)/shard_map/pallas_call | solution.py:220
  125.6 3.0 %collective-permute-done.26 = bf16[192,384]{1,0:T(8,128)(2,1)S(1)} collective-permute-done((bf16[192,384]{1,0:T(8,128)(2,1)S(1)}, bf16[192,384]{1,0:T(8,128)(2,1)S(1)}, u32[]{:S(2)}, u32[]{:S(2)}) %collective-permute-start.26) | collective-permute-done | bytes 147488 | tf_op jit(solution)/shard_map/ppermute | solution.py:23
  128.7 4.8 %collective-permute-start.36 = (bf16[192,384]{1,0:T(8,128)(2,1)S(1)}, bf16[192,384]{1,0:T(8,128)(2,1)S(1)}, u32[]{:S(2)}, u32[]{:S(2)}) collective-permute-start(bf16[192,384]{1,0:T(8,128)(2,1)S(1)} %fusion.refs_8_), channel_id=1, source_target_pairs={{0,192},{1,193},{2,194},{3,195},{4,196},{5,197},{6,198},{7,199},{8... | collective-permute-start | bytes 442376 | tf_op jit(solution)/shard_map/ppermute | solution.py:23
  133.6 3.5 %collective-permute-done.36.refs_10_ = bf16[192,384]{1,0:T(8,128)(2,1)S(1)} collective-permute-done((bf16[192,384]{1,0:T(8,128)(2,1)S(1)}, bf16[192,384]{1,0:T(8,128)(2,1)S(1)}, u32[]{:S(2)}, u32[]{:S(2)}) %collective-permute-start.36) | collective-permute-done | bytes 147488 | tf_op jit(solution)/shard_map/ppermute | solution.py:23
  137.1 4.3 %collective-permute-start.37 = (bf16[192,384]{1,0:T(8,128)(2,1)S(1)}, bf16[192,384]{1,0:T(8,128)(2,1)S(1)}, u32[]{:S(2)}, u32[]{:S(2)}) collective-permute-start(bf16[192,384]{1,0:T(8,128)(2,1)S(1)} %collective-permute-done.36.refs_10_), channel_id=1, source_target_pairs={{0,192},{1,193},{2,194},{3,195},{4,196},{5,197},{6,198},{7,199},{8... | collective-permute-start | bytes 442376 | tf_op jit(solution)/shard_map/ppermute | solution.py:23
  141.6 7.5 %collective-permute-start.38 = (bf16[192,384]{1,0:T(8,128)(2,1)S(1)}, bf16[192,384]{1,0:T(8,128)(2,1)S(1)}, u32[]{:S(2)}, u32[]{:S(2)}) collective-permute-start(bf16[192,384]{1,0:T(8,128)(2,1)S(1)} %fusion.refs_8_), channel_id=1, source_target_pairs={{0,32},{1,33},{2,34},{3,35},{4,36},{5,37},{6,38},{7,39},{8,40},{9,... | collective-permute-start | bytes 442376 | tf_op jit(solution)/shard_map/ppermute | solution.py:23
  150.1 4.8 %collective-permute-start.28 = (bf16[208,384]{1,0:T(8,128)(2,1)S(1)}, bf16[208,384]{1,0:T(8,128)(2,1)S(1)}, u32[]{:S(2)}, u32[]{:S(2)}) collective-permute-start(bf16[208,384]{1,0:T(8,128)(2,1)S(1)} %pad_maximum_fusion.refs_8_.refs_0_), channel_id=1, source_target_pairs={{0,192},{1,193},{2,194},{3,195},{4,196},{5,197},{6,198},{7,199},{8... | collective-permute-start | bytes 479240 | tf_op jit(solution)/shard_map/ppermute | solution.py:23
  154.9 3.2 %shard_map.98 = bf16[192,768]{1,0:T(8,128)(2,1)S(1)} custom-call(bf16[4,2,96,384]{3,2,1,0:T(8,128)(2,1)S(1)} %get-tuple-element.25.refs_0_, bf16[4,2,96,384]{3,2,1,0:T(8,128)(2,1)S(1)} %collective-permute-done.3.refs_1_, bf16[4,2,96,384]{3,2,1,0:T(8,128)(2,1)S(1)} %collective-permute-done.4.refs_2_, ...), custom_call_target="tpu_custom_call" | custom-call | flops 905969664 | bytes 5000000 | tf_op jit(solution)/shard_map/pallas_call | solution.py:220
  161.2 4.4 %collective-permute-done.29.refs_11_.refs_3_ = bf16[208,384]{1,0:T(8,128)(2,1)S(1)} collective-permute-done((bf16[208,384]{1,0:T(8,128)(2,1)S(1)}, bf16[208,384]{1,0:T(8,128)(2,1)S(1)}, u32[]{:S(2)}, u32[]{:S(2)}) %collective-permute-start.29) | collective-permute-done | bytes 159776 | tf_op jit(solution)/shard_map/ppermute | solution.py:23
  167.2 3.2 %shard_map.97 = f32[192,768]{1,0:T(8,128)S(1)} custom-call(bf16[4,2,96,384]{3,2,1,0:T(8,128)(2,1)S(1)} %get-tuple-element.25.refs_0_, bf16[4,2,96,384]{3,2,1,0:T(8,128)(2,1)S(1)} %collective-permute-done.3.refs_1_, bf16[4,2,96,384]{3,2,1,0:T(8,128)(2,1)S(1)} %collective-permute-done.4.refs_2_, bf16[4,2,96,384]{3,2,1,0:T(8,128)(2,1)S(1)} %collective-permute-done.5.refs_3_, ...), custom_call_target="tpu_custom_call" | custom-call | flops 905969664 | bytes 5000000 | tf_op jit(solution)/shard_map/pallas_call | solution.py:220
  (155 shorter events, 58.5 us)
Async XLA Ops:
  6.8 14.0 %collective-permute-start.8 = (bf16[4,96,384]{2,1,0:T(8,128)(2,1)}, bf16[4,96,384]{2,1,0:T(8,128)(2,1)S(1)}, u32[]{:S(2)}, u32[]{:S(2)}) collective-permute-start(bf16[4,96,384]{2,1,0:T(8,128)(2,1)} %get-tuple-element.26.a), channel_id=1, source_target_pairs={{0,16},{1,17},{2,18},{3,19},{4,20},{5,21},{6,22},{7,23},{8,24},{9,... | collective-permute-start | bytes 884744 | tf_op jit(solution)/shard_map/ppermute | solution.py:23
  8.3 17.5 %collective-permute-start.18 = (bf16[2,192,384]{2,1,0:T(8,128)(2,1)}, bf16[2,192,384]{2,1,0:T(8,128)(2,1)S(1)}, u32[]{:S(2)}, u32[]{:S(2)}) collective-permute-start(bf16[2,192,384]{2,1,0:T(8,128)(2,1)} %get-tuple-element.32), channel_id=1, source_target_pairs={{0,1},{1,0},{2,3},{3,2},{4,5},{5,4},{6,7},{7,6},{8,9},{9,8},{10,11... | collective-permute-start | bytes 884744 | tf_op jit(solution)/shard_map/ppermute | solution.py:23
  10.0 23.6 %collective-permute-start = (bf16[4,96,384]{2,1,0:T(8,128)(2,1)}, bf16[4,96,384]{2,1,0:T(8,128)(2,1)S(1)}, u32[]{:S(2)}, u32[]{:S(2)}) collective-permute-start(bf16[4,96,384]{2,1,0:T(8,128)(2,1)} %get-tuple-element.24.a), channel_id=1, source_target_pairs={{0,2},{1,3},{2,4},{3,5},{4,6},{5,7},{6,0},{7,1},{8,10},{9,11},{10,... | collective-permute-start | bytes 884744 | tf_op jit(solution)/shard_map/ppermute | solution.py:23
  11.7 21.8 %collective-permute-start.1 = (bf16[4,96,384]{2,1,0:T(8,128)(2,1)}, bf16[4,96,384]{2,1,0:T(8,128)(2,1)S(1)}, u32[]{:S(2)}, u32[]{:S(2)}) collective-permute-start(bf16[4,96,384]{2,1,0:T(8,128)(2,1)} %get-tuple-element.24.a), channel_id=1, source_target_pairs={{0,6},{1,7},{2,0},{3,1},{4,2},{5,3},{6,4},{7,5},{8,14},{9,15},{10,... | collective-permute-start | bytes 884744 | tf_op jit(solution)/shard_map/ppermute | solution.py:23
  22.0 26.3 %collective-permute-start.15 = (bf16[4,2,96,384]{3,2,1,0:T(8,128)(2,1)S(1)}, bf16[4,2,96,384]{3,2,1,0:T(8,128)(2,1)S(1)}, u32[]{:S(2)}, u32[]{:S(2)}) collective-permute-start(bf16[4,2,96,384]{3,2,1,0:T(8,128)(2,1)S(1)} %get-tuple-element.30.refs_4_), channel_id=1, source_target_pairs={{0,2},{1,3},{2,4},{3,5},{4,6},{5,7},{6,0},{7,1},{8,10},{9,11},{10,... | collective-permute-start | bytes 1769480 | tf_op jit(solution)/shard_map/ppermute | solution.py:23
  23.3 20.8 %collective-permute-start.2 = (bf16[4,96,384]{2,1,0:T(8,128)(2,1)}, bf16[4,96,384]{2,1,0:T(8,128)(2,1)S(1)}, u32[]{:S(2)}, u32[]{:S(2)}) collective-permute-start(bf16[4,96,384]{2,1,0:T(8,128)(2,1)} %get-tuple-element.24.a), channel_id=1, source_target_pairs={{0,4},{1,5},{2,6},{3,7},{4,0},{5,1},{6,2},{7,3},{8,12},{9,13},{10,... | collective-permute-start | bytes 884744 | tf_op jit(solution)/shard_map/ppermute | solution.py:23
  27.5 16.9 %collective-permute-start.20 = (bf16[384,384]{1,0:T(8,128)(2,1)S(1)}, bf16[384,384]{1,0:T(8,128)(2,1)S(1)}, u32[]{:S(2)}, u32[]{:S(2)}) collective-permute-start(bf16[384,384]{1,0:T(8,128)(2,1)S(1)} %join.1.refs_8_), channel_id=1, source_target_pairs={{0,192},{1,193},{2,194},{3,195},{4,196},{5,197},{6,198},{7,199},{8... | collective-permute-start | bytes 884744 | tf_op jit(solution)/shard_map/ppermute | solution.py:23
  44.4 19.0 %collective-permute-start.17 = (bf16[4,2,96,384]{3,2,1,0:T(8,128)(2,1)S(1)}, bf16[4,2,96,384]{3,2,1,0:T(8,128)(2,1)S(1)}, u32[]{:S(2)}, u32[]{:S(2)}) collective-permute-start(bf16[4,2,96,384]{3,2,1,0:T(8,128)(2,1)S(1)} %get-tuple-element.30.refs_4_), channel_id=1, source_target_pairs={{0,4},{1,5},{2,6},{3,7},{4,0},{5,1},{6,2},{7,3},{8,12},{9,13},{10,... | collective-permute-start | bytes 1769480 | tf_op jit(solution)/shard_map/ppermute | solution.py:23
  45.0 27.6 %collective-permute-start.12 = (bf16[4,2,96,384]{3,2,1,0:T(8,128)(2,1)S(1)}, bf16[4,2,96,384]{3,2,1,0:T(8,128)(2,1)S(1)}, u32[]{:S(2)}, u32[]{:S(2)}) collective-permute-start(bf16[4,2,96,384]{3,2,1,0:T(8,128)(2,1)S(1)} %get-tuple-element.29.refs_0_), channel_id=1, source_target_pairs={{0,8},{1,9},{2,10},{3,11},{4,12},{5,13},{6,14},{7,15},{8,16},{9,17... | collective-permute-start | bytes 1769480 | tf_op jit(solution)/shard_map/ppermute | solution.py:23
  46.0 27.4 %collective-permute-start.13 = (bf16[4,2,96,384]{3,2,1,0:T(8,128)(2,1)S(1)}, bf16[4,2,96,384]{3,2,1,0:T(8,128)(2,1)S(1)}, u32[]{:S(2)}, u32[]{:S(2)}) collective-permute-start(bf16[4,2,96,384]{3,2,1,0:T(8,128)(2,1)S(1)} %get-tuple-element.29.refs_0_), channel_id=1, source_target_pairs={{0,24},{1,25},{2,26},{3,27},{4,28},{5,29},{6,30},{7,31},{8,0},{9,1... | collective-permute-start | bytes 1769480 | tf_op jit(solution)/shard_map/ppermute | solution.py:23
  49.2 29.7 %collective-permute-start.14 = (bf16[4,2,96,384]{3,2,1,0:T(8,128)(2,1)S(1)}, bf16[4,2,96,384]{3,2,1,0:T(8,128)(2,1)S(1)}, u32[]{:S(2)}, u32[]{:S(2)}) collective-permute-start(bf16[4,2,96,384]{3,2,1,0:T(8,128)(2,1)S(1)} %get-tuple-element.29.refs_0_), channel_id=1, source_target_pairs={{0,16},{1,17},{2,18},{3,19},{4,20},{5,21},{6,22},{7,23},{8,24},{9,... | collective-permute-start | bytes 1769480 | tf_op jit(solution)/shard_map/ppermute | solution.py:23
  57.5 22.2 %collective-permute-start.21 = (bf16[384,384]{1,0:T(8,128)(2,1)S(1)}, bf16[384,384]{1,0:T(8,128)(2,1)}, u32[]{:S(2)}, u32[]{:S(2)}) collective-permute-start(bf16[384,384]{1,0:T(8,128)(2,1)S(1)} %collective-permute-done.20.refs_10_), channel_id=1, source_target_pairs={{0,192},{1,193},{2,194},{3,195},{4,196},{5,197},{6,198},{7,199},{8... | collective-permute-start | bytes 884744 | tf_op jit(solution)/shard_map/ppermute | solution.py:23
  64.2 57.1 %collective-permute-start.10 = (bf16[4,2,96,384]{3,2,1,0:T(8,128)(2,1)S(1)}, bf16[4,2,96,384]{3,2,1,0:T(8,128)(2,1)S(1)}, u32[]{:S(2)}, u32[]{:S(2)}) collective-permute-start(bf16[4,2,96,384]{3,2,1,0:T(8,128)(2,1)S(1)} %get-tuple-element.27.refs_4_), channel_id=1, source_target_pairs={{0,6},{1,7},{2,0},{3,1},{4,2},{5,3},{6,4},{7,5},{8,14},{9,15},{10,... | collective-permute-start | bytes 1769480 | tf_op jit(solution)/shard_map/ppermute | solution.py:23
  73.4 49.5 %collective-permute-start.11 = (bf16[4,2,96,384]{3,2,1,0:T(8,128)(2,1)S(1)}, bf16[4,2,96,384]{3,2,1,0:T(8,128)(2,1)S(1)}, u32[]{:S(2)}, u32[]{:S(2)}) collective-permute-start(bf16[4,2,96,384]{3,2,1,0:T(8,128)(2,1)S(1)} %get-tuple-element.27.refs_4_), channel_id=1, source_target_pairs={{0,4},{1,5},{2,6},{3,7},{4,0},{5,1},{6,2},{7,3},{8,12},{9,13},{10,... | collective-permute-start | bytes 1769480 | tf_op jit(solution)/shard_map/ppermute | solution.py:23
  74.2 16.6 %collective-permute-start.24 = (bf16[384,384]{1,0:T(8,128)(2,1)S(1)}, bf16[384,384]{1,0:T(8,128)(2,1)}, u32[]{:S(2)}, u32[]{:S(2)}) collective-permute-start(bf16[384,384]{1,0:T(8,128)(2,1)S(1)} %collective-permute-done.20.refs_10_), channel_id=1, source_target_pairs={{0,32},{1,33},{2,34},{3,35},{4,36},{5,37},{6,38},{7,39},{8,40},{9,... | collective-permute-start | bytes 884744 | tf_op jit(solution)/shard_map/ppermute | solution.py:23
  82.8 23.4 %all-to-all-start = ((f32[32,4,128]{2,1,0:T(4,128)}), f32[32,4,128]{2,1,0:T(4,128)}, u32[]{:S(2)}, u32[]{:S(2)}) async-start(f32[32,4,128]{2,1,0:T(4,128)} %copy-done.31), calls=%async_computation | async-start | bytes 131072 | tf_op jit(solution)/shard_map/all_to_all | solution.py:342
  103.9 20.5 %collective-permute-start.34 = (bf16[192,384]{1,0:T(8,128)(2,1)}, bf16[192,384]{1,0:T(8,128)(2,1)}, u32[]{:S(2)}, u32[]{:S(2)}) collective-permute-start(bf16[192,384]{1,0:T(8,128)(2,1)} %get-tuple-element.37), channel_id=1, source_target_pairs={{0,1},{1,0},{2,3},{3,2},{4,5},{5,4},{6,7},{7,6},{8,9},{9,8},{10,11... | collective-permute-start | bytes 442376 | tf_op jit(solution)/shard_map/ppermute | solution.py:23
  105.1 28.4 %collective-permute-start.9 = (bf16[4,2,96,384]{3,2,1,0:T(8,128)(2,1)S(1)}, bf16[4,2,96,384]{3,2,1,0:T(8,128)(2,1)S(1)}, u32[]{:S(2)}, u32[]{:S(2)}) collective-permute-start(bf16[4,2,96,384]{3,2,1,0:T(8,128)(2,1)S(1)} %get-tuple-element.27.refs_4_), channel_id=1, source_target_pairs={{0,2},{1,3},{2,4},{3,5},{4,6},{5,7},{6,0},{7,1},{8,10},{9,11},{10,... | collective-permute-start | bytes 1769480 | tf_op jit(solution)/shard_map/ppermute | solution.py:23
  107.1 34.3 %collective-permute-start.3 = (bf16[4,2,96,384]{3,2,1,0:T(8,128)(2,1)S(1)}, bf16[4,2,96,384]{3,2,1,0:T(8,128)(2,1)S(1)}, u32[]{:S(2)}, u32[]{:S(2)}) collective-permute-start(bf16[4,2,96,384]{3,2,1,0:T(8,128)(2,1)S(1)} %get-tuple-element.25.refs_0_), channel_id=1, source_target_pairs={{0,8},{1,9},{2,10},{3,11},{4,12},{5,13},{6,14},{7,15},{8,16},{9,17... | collective-permute-start | bytes 1769480 | tf_op jit(solution)/shard_map/ppermute | solution.py:23
  121.3 20.2 %collective-permute-start.4 = (bf16[4,2,96,384]{3,2,1,0:T(8,128)(2,1)S(1)}, bf16[4,2,96,384]{3,2,1,0:T(8,128)(2,1)S(1)}, u32[]{:S(2)}, u32[]{:S(2)}) collective-permute-start(bf16[4,2,96,384]{3,2,1,0:T(8,128)(2,1)S(1)} %get-tuple-element.25.refs_0_), channel_id=1, source_target_pairs={{0,24},{1,25},{2,26},{3,27},{4,28},{5,29},{6,30},{7,31},{8,0},{9,1... | collective-permute-start | bytes 1769480 | tf_op jit(solution)/shard_map/ppermute | solution.py:23
  122.9 26.2 %collective-permute-start.5 = (bf16[4,2,96,384]{3,2,1,0:T(8,128)(2,1)S(1)}, bf16[4,2,96,384]{3,2,1,0:T(8,128)(2,1)S(1)}, u32[]{:S(2)}, u32[]{:S(2)}) collective-permute-start(bf16[4,2,96,384]{3,2,1,0:T(8,128)(2,1)S(1)} %get-tuple-element.25.refs_0_), channel_id=1, source_target_pairs={{0,16},{1,17},{2,18},{3,19},{4,20},{5,21},{6,22},{7,23},{8,24},{9,... | collective-permute-start | bytes 1769480 | tf_op jit(solution)/shard_map/ppermute | solution.py:23
  133.5 15.6 %collective-permute-start.35 = (bf16[192,384]{1,0:T(8,128)(2,1)S(1)}, bf16[192,384]{1,0:T(8,128)(2,1)S(1)}, u32[]{:S(2)}, u32[]{:S(2)}) collective-permute-start(bf16[192,384]{1,0:T(8,128)(2,1)S(1)} %fusion.refs_8_), channel_id=1, source_target_pairs={{0,64},{1,65},{2,66},{3,67},{4,68},{5,69},{6,70},{7,71},{8,72},{9,... | collective-permute-start | bytes 442376 | tf_op jit(solution)/shard_map/ppermute | solution.py:23
  141.5 13.4 %collective-permute-start.27 = (bf16[208,384]{1,0:T(8,128)(2,1)S(1)}, bf16[208,384]{1,0:T(8,128)(2,1)S(1)}, u32[]{:S(2)}, u32[]{:S(2)}) collective-permute-start(bf16[208,384]{1,0:T(8,128)(2,1)S(1)} %pad_maximum_fusion.refs_8_.refs_0_), channel_id=1, source_target_pairs={{0,64},{1,65},{2,66},{3,67},{4,68},{5,69},{6,70},{7,71},{8,72},{9,... | collective-permute-start | bytes 479240 | tf_op jit(solution)/shard_map/ppermute | solution.py:23
  158.1 13.1 %collective-permute-start.42 = (bf16[192,768]{1,0:T(8,128)(2,1)S(1)}, bf16[192,768]{1,0:T(8,128)(2,1)S(1)}, u32[]{:S(2)}, u32[]{:S(2)}) collective-permute-start(bf16[192,768]{1,0:T(8,128)(2,1)S(1)} %shard_map.98), channel_id=1, source_target_pairs={{0,1},{1,0},{2,3},{3,2},{4,5},{5,4},{6,7},{7,6},{8,9},{9,8},{10,11... | collective-permute-start | bytes 884744 | tf_op jit(solution)/shard_map/ppermute | solution.py:23
  (58 other events, 495.3 us)

commit v4 on v3

--- a/solution.py
+++ b/solution.py
@@ -169,22 +169,6 @@
     count = g.shape[1]
     sides = ((0 if sending else 1),) if stage == 1 else (0, 1)
 
-    @pl.loop(0, 4)
-    def _(inner):
-        di = jnp.where(inner < 2, 3 * inner, inner - 1)
-        for outer, ds in enumerate(STEPS):
-            for half in range(2):
-                dy, dx = (ds, di) if half == 0 else (di, ds)
-                at_y, at_x = lax.rem(y + dy + 4, 4), lax.rem(x + dx + 4, 4)
-                row = pl.multiple_of((at_y * 4 + at_x) * 192 + half * 96, 32)
-                for at, side in enumerate(sides):
-                    for lane in (0, 128, 256):
-                        pltpu.make_async_copy(
-                            stacks[4 * half + outer].at[inner, side, :, pl.ds(lane, 128)],
-                            w.at[pl.ds(row, 96), pl.ds(at * 384 + lane, 128)],
-                            w_sems.at[at_y],
-                        ).start()
-
     for i, dz in enumerate(STEPS):
         for other in range(2):
             at_z, at_core = lax.rem(zh + dz + 4, 4), lax.rem(core + other, 2)
@@ -193,10 +177,27 @@
                 g.at[at_z, :, pl.ds(pl.multiple_of(at_core * 384, 128), 384)],
                 g_sems.at[at_z],
             ).start()
+    chunks = ((0, 128), (128, 256)) if stage == 1 else ((0, 384),)
+    for down, dy in enumerate(STEPS):
+        at_y = lax.rem(y + dy + 4, 4)
+        for along, dx in enumerate(STEPS):
+            row = (at_y * 4 + lax.rem(x + dx + 4, 4)) * 192
+            for half in range(2):
+                block = stacks[4 + along].at[down] if half else stacks[down].at[along]
+                into = pl.ds(pl.multiple_of(row + half * 96, 32), 96)
+                for at, side in enumerate(sides):
+                    for lane, size in chunks:
+                        pltpu.make_async_copy(
+                            block.at[side, :, pl.ds(lane, size)],
+                            w.at[into, pl.ds(at * 384 + lane, size)],
+                            w_sems.at[at_y],
+                        ).start()
+
     total[...] = jnp.zeros_like(total)
 
     @pl.loop(0, 4)
-    def _(k):
+    def _(down):
+        k = lax.rem(y + jnp.where(down < 2, 3 * down, down - 1), 4)
         part = pl.ds(pl.multiple_of(k * 768, 768), 768)
         pltpu.make_async_copy(w.at[part, :], w.at[part, :], w_sems.at[k]).wait()
         pltpu.make_async_copy(g.at[k], g.at[k], g_sems.at[k]).wait()

time: 173 us -> 172 us (level)
  Pallas kernels: 19.6 us -> 17.4 us
    pallas_call x4, Pallas kernels: 13.8 us -> 11.7 us  [product(): pl.pallas_call(functools.partial(product_kernel, stage, sending), out_sha...]
  transfers between devices with their start and end apart: 44 -> 44, of which waited for: 10 -> 9; matrix products, arithmetic and copies ran while one was open for 1% -> 1% of each run, Pallas kernels for 10% -> 9%
where the time goes in v4:
time: 172 us; the launch traced here: 171 us
  starting transfers between devices  88.3 us (51%)
  waiting for transfers between devices  33 us (19%)
  local copies, waits for them, and re-layouts  29.1 us (17%)
  Pallas kernels  17.4 us (10%)
  other arithmetic  1.9 us (1%)
    ppermute x43, starting transfers between devices, shift(): return lax.ppermute(value, ('row', 'col'), pairs)  80.4 us
    ppermute x43, waiting for transfers between devices, shift(): return lax.ppermute(value, ('row', 'col'), pairs)  33 us
    unnamed x76, local copies, waits for them, and re-layouts  29.1 us
    pallas_call x4, Pallas kernels, product(): pl.pallas_call(functools.partial(product_kernel, stage, sending), out_sha...  11.7 us
    all_to_all x1, starting transfers between devices, on_device(): parts = lax.all_to_all(parts, 'col', 0, 0)  7.89 us
  transfers between devices with their start and end apart: 44, of which 9 were waited for; matrix products, arithmetic and copies ran while one was open for 1% of the time, Pallas kernels for 9%

profile of v4, /device:TPU:1, one launch (start us, length us, event | category | flops | bytes accessed | tf_op | source)
XLA Modules:
  0.0 170.7 jit_solution(16375851379704058097)
XLA Ops:
  0.6 2.4 %prepare.1 = (bf16[4,96,384]{2,1,0:T(8,128)(2,1)}, bf16[4,96,384]{2,1,0:T(8,128)(2,1)}, bf16[192,384]{1,0:T(8,128)(2,1)}, bf16[192,384]{1,0:T(8,128)(2,1)}, bf16[2,192,384]{2,1,0:T(8,128)(2,1)}) custom-call(bf16[192,768]{1,0:T(8,128)(2,1)} %bitcast.12, bf16[192,768]{1,0:T(8,128)(2,1)} %bitcast.13, bf16[192,768]{1,0:T(8,128)(2,1)} %bitcast.14, ...), custom_call_target="tpu_custom_call" | custom-call | flops 1000000 | bytes 2000000 | tf_op jit(solution)/shard_map/prepare/pallas_call | solution.py:93
  11.7 4.2 %collective-permute-start.1 = (bf16[4,96,384]{2,1,0:T(8,128)(2,1)}, bf16[4,96,384]{2,1,0:T(8,128)(2,1)S(1)}, u32[]{:S(2)}, u32[]{:S(2)}) collective-permute-start(bf16[4,96,384]{2,1,0:T(8,128)(2,1)} %get-tuple-element.24.a), channel_id=1, source_target_pairs={{0,6},{1,7},{2,0},{3,1},{4,2},{5,3},{6,4},{7,5},{8,14},{9,15},{10,... | collective-permute-start | bytes 884744 | tf_op jit(solution)/shard_map/ppermute | solution.py:23
  15.9 5.0 %collective-permute-done.8.d = bf16[4,96,384]{2,1,0:T(8,128)(2,1)S(1)} collective-permute-done((bf16[4,96,384]{2,1,0:T(8,128)(2,1)}, bf16[4,96,384]{2,1,0:T(8,128)(2,1)S(1)}, u32[]{:S(2)}, u32[]{:S(2)}) %collective-permute-start.8) | collective-permute-done | bytes 294944 | tf_op jit(solution)/shard_map/ppermute | solution.py:23
  23.3 2.5 %collective-permute-start.2 = (bf16[4,96,384]{2,1,0:T(8,128)(2,1)}, bf16[4,96,384]{2,1,0:T(8,128)(2,1)S(1)}, u32[]{:S(2)}, u32[]{:S(2)}) collective-permute-start(bf16[4,96,384]{2,1,0:T(8,128)(2,1)} %get-tuple-element.24.a), channel_id=1, source_target_pairs={{0,4},{1,5},{2,6},{3,7},{4,0},{5,1},{6,2},{7,3},{8,12},{9,13},{10,... | collective-permute-start | bytes 884744 | tf_op jit(solution)/shard_map/ppermute | solution.py:23
  27.5 6.0 %collective-permute-start.20 = (bf16[384,384]{1,0:T(8,128)(2,1)S(1)}, bf16[384,384]{1,0:T(8,128)(2,1)S(1)}, u32[]{:S(2)}, u32[]{:S(2)}) collective-permute-start(bf16[384,384]{1,0:T(8,128)(2,1)S(1)} %join.1.refs_8_), channel_id=1, source_target_pairs={{0,192},{1,193},{2,194},{3,195},{4,196},{5,197},{6,198},{7,199},{8... | collective-permute-start | bytes 884744 | tf_op jit(solution)/shard_map/ppermute | solution.py:23
  33.5 2.5 %collective-permute-start.22 = (bf16[384,384]{1,0:T(8,128)(2,1)S(1)}, bf16[384,384]{1,0:T(8,128)(2,1)S(1)}, u32[]{:S(2)}, u32[]{:S(2)}) collective-permute-start(bf16[384,384]{1,0:T(8,128)(2,1)S(1)} %join.1.refs_8_), channel_id=1, source_target_pairs={{0,32},{1,33},{2,34},{3,35},{4,36},{5,37},{6,38},{7,39},{8,40},{9,... | collective-permute-start | bytes 884744 | tf_op jit(solution)/shard_map/ppermute | solution.py:23
  36.0 8.1 %collective-permute-done.2.d = bf16[4,96,384]{2,1,0:T(8,128)(2,1)S(1)} collective-permute-done((bf16[4,96,384]{2,1,0:T(8,128)(2,1)}, bf16[4,96,384]{2,1,0:T(8,128)(2,1)S(1)}, u32[]{:S(2)}, u32[]{:S(2)}) %collective-permute-start.2) | collective-permute-done | bytes 294944 | tf_op jit(solution)/shard_map/ppermute | solution.py:23
  50.0 6.7 %collective-permute-done.16.refs_6_ = bf16[4,2,96,384]{3,2,1,0:T(8,128)(2,1)S(1)} collective-permute-done((bf16[4,2,96,384]{3,2,1,0:T(8,128)(2,1)S(1)}, bf16[4,2,96,384]{3,2,1,0:T(8,128)(2,1)S(1)}, u32[]{:S(2)}, u32[]{:S(2)}) %collective-permute-start.16) | collective-permute-done | bytes 589856 | tf_op jit(solution)/shard_map/ppermute | solution.py:23
  57.5 5.8 %collective-permute-start.21 = (bf16[384,384]{1,0:T(8,128)(2,1)S(1)}, bf16[384,384]{1,0:T(8,128)(2,1)}, u32[]{:S(2)}, u32[]{:S(2)}) collective-permute-start(bf16[384,384]{1,0:T(8,128)(2,1)S(1)} %collective-permute-done.20.refs_10_), channel_id=1, source_target_pairs={{0,192},{1,193},{2,194},{3,195},{4,196},{5,197},{6,198},{7,199},{8... | collective-permute-start | bytes 884744 | tf_op jit(solution)/shard_map/ppermute | solution.py:23
  64.2 8.4 %collective-permute-start.10 = (bf16[4,2,96,384]{3,2,1,0:T(8,128)(2,1)S(1)}, bf16[4,2,96,384]{3,2,1,0:T(8,128)(2,1)S(1)}, u32[]{:S(2)}, u32[]{:S(2)}) collective-permute-start(bf16[4,2,96,384]{3,2,1,0:T(8,128)(2,1)S(1)} %get-tuple-element.27.refs_4_), channel_id=1, source_target_pairs={{0,6},{1,7},{2,0},{3,1},{4,2},{5,3},{6,4},{7,5},{8,14},{9,15},{10,... | collective-permute-start | bytes 1769480 | tf_op jit(solution)/shard_map/ppermute | solution.py:23
  74.2 4.7 %collective-permute-start.24 = (bf16[384,384]{1,0:T(8,128)(2,1)S(1)}, bf16[384,384]{1,0:T(8,128)(2,1)}, u32[]{:S(2)}, u32[]{:S(2)}) collective-permute-start(bf16[384,384]{1,0:T(8,128)(2,1)S(1)} %collective-permute-done.20.refs_10_), channel_id=1, source_target_pairs={{0,32},{1,33},{2,34},{3,35},{4,36},{5,37},{6,38},{7,39},{8,40},{9,... | collective-permute-start | bytes 884744 | tf_op jit(solution)/shard_map/ppermute | solution.py:23
  82.8 7.9 %all-to-all-start = ((f32[32,4,128]{2,1,0:T(4,128)}), f32[32,4,128]{2,1,0:T(4,128)}, u32[]{:S(2)}, u32[]{:S(2)}) async-start(f32[32,4,128]{2,1,0:T(4,128)} %copy-done.31), calls=%async_computation | async-start | bytes 131072 | tf_op jit(solution)/shard_map/all_to_all | solution.py:343
  99.2 3.3 %shard_map.96 = (bf16[192,384]{1,0:T(8,128)(2,1)}, bf16[192,384]{1,0:T(8,128)(2,1)S(1)}) custom-call(bf16[4,2,96,384]{3,2,1,0:T(8,128)(2,1)S(1)} %copy-done.9, bf16[4,2,96,384]{3,2,1,0:T(8,128)(2,1)S(1)} %copy-done.15, bf16[4,2,96,384]{3,2,1,0:T(8,128)(2,1)S(1)} %copy-done.18, bf16[4,2,96,384]{3,2,1,0:T(8,128)(2,1)S(1)} %copy-done.21, ...), custom_call_target="tpu_custom_call" | custom-call | flops 905969664 | bytes 5000000 | tf_op jit(solution)/shard_map/pallas_call | solution.py:221
  117.7 2.7 %shard_map.95 = (f32[192,384]{1,0:T(8,128)S(1)}, f32[192,384]{1,0:T(8,128)S(1)}) custom-call(bf16[4,2,96,384]{3,2,1,0:T(8,128)(2,1)S(1)} %copy-done.10, bf16[4,2,96,384]{3,2,1,0:T(8,128)(2,1)S(1)} %copy-done.16, bf16[4,2,96,384]{3,2,1,0:T(8,128)(2,1)S(1)} %copy-done.19, bf16[4,2,96,384]{3,2,1,0:T(8,128)(2,1)S(1)} %copy-done.22, ...), custom_call_target="tpu_custom_call" | custom-call | flops 905969664 | bytes 5000000 | tf_op jit(solution)/shard_map/pallas_call | solution.py:221
  125.5 3.0 %collective-permute-done.26 = bf16[192,384]{1,0:T(8,128)(2,1)S(1)} collective-permute-done((bf16[192,384]{1,0:T(8,128)(2,1)S(1)}, bf16[192,384]{1,0:T(8,128)(2,1)S(1)}, u32[]{:S(2)}, u32[]{:S(2)}) %collective-permute-start.26) | collective-permute-done | bytes 147488 | tf_op jit(solution)/shard_map/ppermute | solution.py:23
  128.5 3.7 %collective-permute-start.36 = (bf16[192,384]{1,0:T(8,128)(2,1)S(1)}, bf16[192,384]{1,0:T(8,128)(2,1)S(1)}, u32[]{:S(2)}, u32[]{:S(2)}) collective-permute-start(bf16[192,384]{1,0:T(8,128)(2,1)S(1)} %fusion.refs_8_), channel_id=1, source_target_pairs={{0,192},{1,193},{2,194},{3,195},{4,196},{5,197},{6,198},{7,199},{8... | collective-permute-start | bytes 442376 | tf_op jit(solution)/shard_map/ppermute | solution.py:23
  132.4 2.9 %collective-permute-done.36.refs_10_ = bf16[192,384]{1,0:T(8,128)(2,1)S(1)} collective-permute-done((bf16[192,384]{1,0:T(8,128)(2,1)S(1)}, bf16[192,384]{1,0:T(8,128)(2,1)S(1)}, u32[]{:S(2)}, u32[]{:S(2)}) %collective-permute-start.36) | collective-permute-done | bytes 147488 | tf_op jit(solution)/shard_map/ppermute | solution.py:23
  135.4 3.5 %collective-permute-start.37 = (bf16[192,384]{1,0:T(8,128)(2,1)S(1)}, bf16[192,384]{1,0:T(8,128)(2,1)S(1)}, u32[]{:S(2)}, u32[]{:S(2)}) collective-permute-start(bf16[192,384]{1,0:T(8,128)(2,1)S(1)} %collective-permute-done.36.refs_10_), channel_id=1, source_target_pairs={{0,192},{1,193},{2,194},{3,195},{4,196},{5,197},{6,198},{7,199},{8... | collective-permute-start | bytes 442376 | tf_op jit(solution)/shard_map/ppermute | solution.py:23
  138.9 7.3 %collective-permute-start.38 = (bf16[192,384]{1,0:T(8,128)(2,1)S(1)}, bf16[192,384]{1,0:T(8,128)(2,1)S(1)}, u32[]{:S(2)}, u32[]{:S(2)}) collective-permute-start(bf16[192,384]{1,0:T(8,128)(2,1)S(1)} %fusion.refs_8_), channel_id=1, source_target_pairs={{0,32},{1,33},{2,34},{3,35},{4,36},{5,37},{6,38},{7,39},{8,40},{9,... | collective-permute-start | bytes 442376 | tf_op jit(solution)/shard_map/ppermute | solution.py:23
  146.8 3.3 %collective-permute-start.41 = (bf16[192,384]{1,0:T(8,128)(2,1)S(1)}, bf16[192,384]{1,0:T(8,128)(2,1)S(1)}, u32[]{:S(2)}, u32[]{:S(2)}) collective-permute-start(bf16[192,384]{1,0:T(8,128)(2,1)S(1)} %collective-permute-done.37.refs_11_), channel_id=1, source_target_pairs={{0,32},{1,33},{2,34},{3,35},{4,36},{5,37},{6,38},{7,39},{8,40},{9,... | collective-permute-start | bytes 442376 | tf_op jit(solution)/shard_map/ppermute | solution.py:23
  150.0 4.3 %collective-permute-start.28 = (bf16[208,384]{1,0:T(8,128)(2,1)S(1)}, bf16[208,384]{1,0:T(8,128)(2,1)S(1)}, u32[]{:S(2)}, u32[]{:S(2)}) collective-permute-start(bf16[208,384]{1,0:T(8,128)(2,1)S(1)} %pad_maximum_fusion.refs_8_.refs_0_), channel_id=1, source_target_pairs={{0,192},{1,193},{2,194},{3,195},{4,196},{5,197},{6,198},{7,199},{8... | collective-permute-start | bytes 479240 | tf_op jit(solution)/shard_map/ppermute | solution.py:23
  154.4 2.8 %shard_map.98 = bf16[192,768]{1,0:T(8,128)(2,1)S(1)} custom-call(bf16[4,2,96,384]{3,2,1,0:T(8,128)(2,1)S(1)} %get-tuple-element.25.refs_0_, bf16[4,2,96,384]{3,2,1,0:T(8,128)(2,1)S(1)} %collective-permute-done.3.refs_1_, bf16[4,2,96,384]{3,2,1,0:T(8,128)(2,1)S(1)} %collective-permute-done.4.refs_2_, ...), custom_call_target="tpu_custom_call" | custom-call | flops 905969664 | bytes 5000000 | tf_op jit(solution)/shard_map/pallas_call | solution.py:221
  160.2 4.3 %collective-permute-done.29.refs_11_.refs_3_ = bf16[208,384]{1,0:T(8,128)(2,1)S(1)} collective-permute-done((bf16[208,384]{1,0:T(8,128)(2,1)S(1)}, bf16[208,384]{1,0:T(8,128)(2,1)S(1)}, u32[]{:S(2)}, u32[]{:S(2)}) %collective-permute-start.29) | collective-permute-done | bytes 159776 | tf_op jit(solution)/shard_map/ppermute | solution.py:23
  166.1 2.8 %shard_map.97 = f32[192,768]{1,0:T(8,128)S(1)} custom-call(bf16[4,2,96,384]{3,2,1,0:T(8,128)(2,1)S(1)} %get-tuple-element.25.refs_0_, bf16[4,2,96,384]{3,2,1,0:T(8,128)(2,1)S(1)} %collective-permute-done.3.refs_1_, bf16[4,2,96,384]{3,2,1,0:T(8,128)(2,1)S(1)} %collective-permute-done.4.refs_2_, bf16[4,2,96,384]{3,2,1,0:T(8,128)(2,1)S(1)} %collective-permute-done.5.refs_3_, ...), custom_call_target="tpu_custom_call" | custom-call | flops 905969664 | bytes 5000000 | tf_op jit(solution)/shard_map/pallas_call | solution.py:221
  (155 shorter events, 61.6 us)
Async XLA Ops:
  6.8 14.0 %collective-permute-start.8 = (bf16[4,96,384]{2,1,0:T(8,128)(2,1)}, bf16[4,96,384]{2,1,0:T(8,128)(2,1)S(1)}, u32[]{:S(2)}, u32[]{:S(2)}) collective-permute-start(bf16[4,96,384]{2,1,0:T(8,128)(2,1)} %get-tuple-element.26.a), channel_id=1, source_target_pairs={{0,16},{1,17},{2,18},{3,19},{4,20},{5,21},{6,22},{7,23},{8,24},{9,... | collective-permute-start | bytes 884744 | tf_op jit(solution)/shard_map/ppermute | solution.py:23
  8.3 17.5 %collective-permute-start.18 = (bf16[2,192,384]{2,1,0:T(8,128)(2,1)}, bf16[2,192,384]{2,1,0:T(8,128)(2,1)S(1)}, u32[]{:S(2)}, u32[]{:S(2)}) collective-permute-start(bf16[2,192,384]{2,1,0:T(8,128)(2,1)} %get-tuple-element.32), channel_id=1, source_target_pairs={{0,1},{1,0},{2,3},{3,2},{4,5},{5,4},{6,7},{7,6},{8,9},{9,8},{10,11... | collective-permute-start | bytes 884744 | tf_op jit(solution)/shard_map/ppermute | solution.py:23
  10.0 23.6 %collective-permute-start = (bf16[4,96,384]{2,1,0:T(8,128)(2,1)}, bf16[4,96,384]{2,1,0:T(8,128)(2,1)S(1)}, u32[]{:S(2)}, u32[]{:S(2)}) collective-permute-start(bf16[4,96,384]{2,1,0:T(8,128)(2,1)} %get-tuple-element.24.a), channel_id=1, source_target_pairs={{0,2},{1,3},{2,4},{3,5},{4,6},{5,7},{6,0},{7,1},{8,10},{9,11},{10,... | collective-permute-start | bytes 884744 | tf_op jit(solution)/shard_map/ppermute | solution.py:23
  11.7 21.8 %collective-permute-start.1 = (bf16[4,96,384]{2,1,0:T(8,128)(2,1)}, bf16[4,96,384]{2,1,0:T(8,128)(2,1)S(1)}, u32[]{:S(2)}, u32[]{:S(2)}) collective-permute-start(bf16[4,96,384]{2,1,0:T(8,128)(2,1)} %get-tuple-element.24.a), channel_id=1, source_target_pairs={{0,6},{1,7},{2,0},{3,1},{4,2},{5,3},{6,4},{7,5},{8,14},{9,15},{10,... | collective-permute-start | bytes 884744 | tf_op jit(solution)/shard_map/ppermute | solution.py:23
  22.0 26.3 %collective-permute-start.15 = (bf16[4,2,96,384]{3,2,1,0:T(8,128)(2,1)S(1)}, bf16[4,2,96,384]{3,2,1,0:T(8,128)(2,1)S(1)}, u32[]{:S(2)}, u32[]{:S(2)}) collective-permute-start(bf16[4,2,96,384]{3,2,1,0:T(8,128)(2,1)S(1)} %get-tuple-element.30.refs_4_), channel_id=1, source_target_pairs={{0,2},{1,3},{2,4},{3,5},{4,6},{5,7},{6,0},{7,1},{8,10},{9,11},{10,... | collective-permute-start | bytes 1769480 | tf_op jit(solution)/shard_map/ppermute | solution.py:23
  23.3 20.8 %collective-permute-start.2 = (bf16[4,96,384]{2,1,0:T(8,128)(2,1)}, bf16[4,96,384]{2,1,0:T(8,128)(2,1)S(1)}, u32[]{:S(2)}, u32[]{:S(2)}) collective-permute-start(bf16[4,96,384]{2,1,0:T(8,128)(2,1)} %get-tuple-element.24.a), channel_id=1, source_target_pairs={{0,4},{1,5},{2,6},{3,7},{4,0},{5,1},{6,2},{7,3},{8,12},{9,13},{10,... | collective-permute-start | bytes 884744 | tf_op jit(solution)/shard_map/ppermute | solution.py:23
  27.5 16.9 %collective-permute-start.20 = (bf16[384,384]{1,0:T(8,128)(2,1)S(1)}, bf16[384,384]{1,0:T(8,128)(2,1)S(1)}, u32[]{:S(2)}, u32[]{:S(2)}) collective-permute-start(bf16[384,384]{1,0:T(8,128)(2,1)S(1)} %join.1.refs_8_), channel_id=1, source_target_pairs={{0,192},{1,193},{2,194},{3,195},{4,196},{5,197},{6,198},{7,199},{8... | collective-permute-start | bytes 884744 | tf_op jit(solution)/shard_map/ppermute | solution.py:23
  44.1 12.6 %collective-permute-start.16 = (bf16[4,2,96,384]{3,2,1,0:T(8,128)(2,1)S(1)}, bf16[4,2,96,384]{3,2,1,0:T(8,128)(2,1)S(1)}, u32[]{:S(2)}, u32[]{:S(2)}) collective-permute-start(bf16[4,2,96,384]{3,2,1,0:T(8,128)(2,1)S(1)} %get-tuple-element.30.refs_4_), channel_id=1, source_target_pairs={{0,6},{1,7},{2,0},{3,1},{4,2},{5,3},{6,4},{7,5},{8,14},{9,15},{10,... | collective-permute-start | bytes 1769480 | tf_op jit(solution)/shard_map/ppermute | solution.py:23
  44.4 19.0 %collective-permute-start.17 = (bf16[4,2,96,384]{3,2,1,0:T(8,128)(2,1)S(1)}, bf16[4,2,96,384]{3,2,1,0:T(8,128)(2,1)S(1)}, u32[]{:S(2)}, u32[]{:S(2)}) collective-permute-start(bf16[4,2,96,384]{3,2,1,0:T(8,128)(2,1)S(1)} %get-tuple-element.30.refs_4_), channel_id=1, source_target_pairs={{0,4},{1,5},{2,6},{3,7},{4,0},{5,1},{6,2},{7,3},{8,12},{9,13},{10,... | collective-permute-start | bytes 1769480 | tf_op jit(solution)/shard_map/ppermute | solution.py:23
  45.0 27.6 %collective-permute-start.12 = (bf16[4,2,96,384]{3,2,1,0:T(8,128)(2,1)S(1)}, bf16[4,2,96,384]{3,2,1,0:T(8,128)(2,1)S(1)}, u32[]{:S(2)}, u32[]{:S(2)}) collective-permute-start(bf16[4,2,96,384]{3,2,1,0:T(8,128)(2,1)S(1)} %get-tuple-element.29.refs_0_), channel_id=1, source_target_pairs={{0,8},{1,9},{2,10},{3,11},{4,12},{5,13},{6,14},{7,15},{8,16},{9,17... | collective-permute-start | bytes 1769480 | tf_op jit(solution)/shard_map/ppermute | solution.py:23
  46.0 27.4 %collective-permute-start.13 = (bf16[4,2,96,384]{3,2,1,0:T(8,128)(2,1)S(1)}, bf16[4,2,96,384]{3,2,1,0:T(8,128)(2,1)S(1)}, u32[]{:S(2)}, u32[]{:S(2)}) collective-permute-start(bf16[4,2,96,384]{3,2,1,0:T(8,128)(2,1)S(1)} %get-tuple-element.29.refs_0_), channel_id=1, source_target_pairs={{0,24},{1,25},{2,26},{3,27},{4,28},{5,29},{6,30},{7,31},{8,0},{9,1... | collective-permute-start | bytes 1769480 | tf_op jit(solution)/shard_map/ppermute | solution.py:23
  49.2 29.7 %collective-permute-start.14 = (bf16[4,2,96,384]{3,2,1,0:T(8,128)(2,1)S(1)}, bf16[4,2,96,384]{3,2,1,0:T(8,128)(2,1)S(1)}, u32[]{:S(2)}, u32[]{:S(2)}) collective-permute-start(bf16[4,2,96,384]{3,2,1,0:T(8,128)(2,1)S(1)} %get-tuple-element.29.refs_0_), channel_id=1, source_target_pairs={{0,16},{1,17},{2,18},{3,19},{4,20},{5,21},{6,22},{7,23},{8,24},{9,... | collective-permute-start | bytes 1769480 | tf_op jit(solution)/shard_map/ppermute | solution.py:23
  57.5 22.2 %collective-permute-start.21 = (bf16[384,384]{1,0:T(8,128)(2,1)S(1)}, bf16[384,384]{1,0:T(8,128)(2,1)}, u32[]{:S(2)}, u32[]{:S(2)}) collective-permute-start(bf16[384,384]{1,0:T(8,128)(2,1)S(1)} %collective-permute-done.20.refs_10_), channel_id=1, source_target_pairs={{0,192},{1,193},{2,194},{3,195},{4,196},{5,197},{6,198},{7,199},{8... | collective-permute-start | bytes 884744 | tf_op jit(solution)/shard_map/ppermute | solution.py:23
  64.2 56.3 %collective-permute-start.10 = (bf16[4,2,96,384]{3,2,1,0:T(8,128)(2,1)S(1)}, bf16[4,2,96,384]{3,2,1,0:T(8,128)(2,1)S(1)}, u32[]{:S(2)}, u32[]{:S(2)}) collective-permute-start(bf16[4,2,96,384]{3,2,1,0:T(8,128)(2,1)S(1)} %get-tuple-element.27.refs_4_), channel_id=1, source_target_pairs={{0,6},{1,7},{2,0},{3,1},{4,2},{5,3},{6,4},{7,5},{8,14},{9,15},{10,... | collective-permute-start | bytes 1769480 | tf_op jit(solution)/shard_map/ppermute | solution.py:23
  73.4 48.8 %collective-permute-start.11 = (bf16[4,2,96,384]{3,2,1,0:T(8,128)(2,1)S(1)}, bf16[4,2,96,384]{3,2,1,0:T(8,128)(2,1)S(1)}, u32[]{:S(2)}, u32[]{:S(2)}) collective-permute-start(bf16[4,2,96,384]{3,2,1,0:T(8,128)(2,1)S(1)} %get-tuple-element.27.refs_4_), channel_id=1, source_target_pairs={{0,4},{1,5},{2,6},{3,7},{4,0},{5,1},{6,2},{7,3},{8,12},{9,13},{10,... | collective-permute-start | bytes 1769480 | tf_op jit(solution)/shard_map/ppermute | solution.py:23
  74.2 16.6 %collective-permute-start.24 = (bf16[384,384]{1,0:T(8,128)(2,1)S(1)}, bf16[384,384]{1,0:T(8,128)(2,1)}, u32[]{:S(2)}, u32[]{:S(2)}) collective-permute-start(bf16[384,384]{1,0:T(8,128)(2,1)S(1)} %collective-permute-done.20.refs_10_), channel_id=1, source_target_pairs={{0,32},{1,33},{2,34},{3,35},{4,36},{5,37},{6,38},{7,39},{8,40},{9,... | collective-permute-start | bytes 884744 | tf_op jit(solution)/shard_map/ppermute | solution.py:23
  82.8 22.7 %all-to-all-start = ((f32[32,4,128]{2,1,0:T(4,128)}), f32[32,4,128]{2,1,0:T(4,128)}, u32[]{:S(2)}, u32[]{:S(2)}) async-start(f32[32,4,128]{2,1,0:T(4,128)} %copy-done.31), calls=%async_computation | async-start | bytes 131072 | tf_op jit(solution)/shard_map/all_to_all | solution.py:343
  103.2 21.1 %collective-permute-start.34 = (bf16[192,384]{1,0:T(8,128)(2,1)}, bf16[192,384]{1,0:T(8,128)(2,1)}, u32[]{:S(2)}, u32[]{:S(2)}) collective-permute-start(bf16[192,384]{1,0:T(8,128)(2,1)} %get-tuple-element.37), channel_id=1, source_target_pairs={{0,1},{1,0},{2,3},{3,2},{4,5},{5,4},{6,7},{7,6},{8,9},{9,8},{10,11... | collective-permute-start | bytes 442376 | tf_op jit(solution)/shard_map/ppermute | solution.py:23
  104.3 28.0 %collective-permute-start.9 = (bf16[4,2,96,384]{3,2,1,0:T(8,128)(2,1)S(1)}, bf16[4,2,96,384]{3,2,1,0:T(8,128)(2,1)S(1)}, u32[]{:S(2)}, u32[]{:S(2)}) collective-permute-start(bf16[4,2,96,384]{3,2,1,0:T(8,128)(2,1)S(1)} %get-tuple-element.27.refs_4_), channel_id=1, source_target_pairs={{0,2},{1,3},{2,4},{3,5},{4,6},{5,7},{6,0},{7,1},{8,10},{9,11},{10,... | collective-permute-start | bytes 1769480 | tf_op jit(solution)/shard_map/ppermute | solution.py:23
  106.4 32.4 %collective-permute-start.3 = (bf16[4,2,96,384]{3,2,1,0:T(8,128)(2,1)S(1)}, bf16[4,2,96,384]{3,2,1,0:T(8,128)(2,1)S(1)}, u32[]{:S(2)}, u32[]{:S(2)}) collective-permute-start(bf16[4,2,96,384]{3,2,1,0:T(8,128)(2,1)S(1)} %get-tuple-element.25.refs_0_), channel_id=1, source_target_pairs={{0,8},{1,9},{2,10},{3,11},{4,12},{5,13},{6,14},{7,15},{8,16},{9,17... | collective-permute-start | bytes 1769480 | tf_op jit(solution)/shard_map/ppermute | solution.py:23
  120.4 18.5 %collective-permute-start.4 = (bf16[4,2,96,384]{3,2,1,0:T(8,128)(2,1)S(1)}, bf16[4,2,96,384]{3,2,1,0:T(8,128)(2,1)S(1)}, u32[]{:S(2)}, u32[]{:S(2)}) collective-permute-start(bf16[4,2,96,384]{3,2,1,0:T(8,128)(2,1)S(1)} %get-tuple-element.25.refs_0_), channel_id=1, source_target_pairs={{0,24},{1,25},{2,26},{3,27},{4,28},{5,29},{6,30},{7,31},{8,0},{9,1... | collective-permute-start | bytes 1769480 | tf_op jit(solution)/shard_map/ppermute | solution.py:23
  122.2 24.1 %collective-permute-start.5 = (bf16[4,2,96,384]{3,2,1,0:T(8,128)(2,1)S(1)}, bf16[4,2,96,384]{3,2,1,0:T(8,128)(2,1)S(1)}, u32[]{:S(2)}, u32[]{:S(2)}) collective-permute-start(bf16[4,2,96,384]{3,2,1,0:T(8,128)(2,1)S(1)} %get-tuple-element.25.refs_0_), channel_id=1, source_target_pairs={{0,16},{1,17},{2,18},{3,19},{4,20},{5,21},{6,22},{7,23},{8,24},{9,... | collective-permute-start | bytes 1769480 | tf_op jit(solution)/shard_map/ppermute | solution.py:23
  132.3 14.0 %collective-permute-start.35 = (bf16[192,384]{1,0:T(8,128)(2,1)S(1)}, bf16[192,384]{1,0:T(8,128)(2,1)S(1)}, u32[]{:S(2)}, u32[]{:S(2)}) collective-permute-start(bf16[192,384]{1,0:T(8,128)(2,1)S(1)} %fusion.refs_8_), channel_id=1, source_target_pairs={{0,64},{1,65},{2,66},{3,67},{4,68},{5,69},{6,70},{7,71},{8,72},{9,... | collective-permute-start | bytes 442376 | tf_op jit(solution)/shard_map/ppermute | solution.py:23
  138.8 15.5 %collective-permute-start.27 = (bf16[208,384]{1,0:T(8,128)(2,1)S(1)}, bf16[208,384]{1,0:T(8,128)(2,1)S(1)}, u32[]{:S(2)}, u32[]{:S(2)}) collective-permute-start(bf16[208,384]{1,0:T(8,128)(2,1)S(1)} %pad_maximum_fusion.refs_8_.refs_0_), channel_id=1, source_target_pairs={{0,64},{1,65},{2,66},{3,67},{4,68},{5,69},{6,70},{7,71},{8,72},{9,... | collective-permute-start | bytes 479240 | tf_op jit(solution)/shard_map/ppermute | solution.py:23
  (58 other events, 499.3 us)
